TPU v7x, 32 devices: a whole 2x2x4 slice. The times are simulated.
32 devices in a mesh: dp: 4 (over z), ctx: 2 (over y), tp: 4 (over x, core).
Axes of the slice: x: 2, y: 2, z: 4, core: 2. Of those that a mesh axis runs over, the one named last changes fastest.
Arguments:
- tokens: float32 [4, 256, 1024], P('dp', 'ctx'), may hold values from -6 to 6
- cotangent: float32 [4, 256, 1024], P('dp', 'ctx'), may hold values from -6 to 6
- doc_lengths: int32 [4, 8], P('dp'), may hold values from 1 to 64, 256 in all within a row
- norm1_gain: float32 [1024], P(('dp', 'ctx')), may hold values from 0.5 to 1.5
- in_weight: float32 [3, 1024, 1024], P(None, ('dp', 'ctx'), 'tp'), may hold values from -0.1875 to 0.1875
- conv_weight: float32 [3, 1024], P(None, 'tp'), may hold values from -3.5 to 3.5
- out_weight: float32 [1024, 1024], P('tp', ('dp', 'ctx')), may hold values from -0.1875 to 0.1875
- norm2_gain: float32 [1024], P(('dp', 'ctx')), may hold values from 0.5 to 1.5
- gate_up_weight: float32 [2, 1024, 4608], P(None, ('dp', 'ctx'), 'tp'), may hold values from -0.1875 to 0.1875
- down_weight: float32 [4608, 1024], P('tp', ('dp', 'ctx')), may hold values from -0.09375 to 0.09375
- first_norm1: float32 [1024], P(('dp', 'ctx')), may hold values from -6 to 6
- first_in: float32 [3, 1024, 1024], P(None, ('dp', 'ctx'), 'tp'), may hold values from -6 to 6
- first_conv: float32 [3, 1024], P(None, 'tp'), may hold values from -6 to 6
- first_out: float32 [1024, 1024], P('tp', ('dp', 'ctx')), may hold values from -6 to 6
- first_norm2: float32 [1024], P(('dp', 'ctx')), may hold values from -6 to 6
- first_gate_up: float32 [2, 1024, 4608], P(None, ('dp', 'ctx'), 'tp'), may hold values from -6 to 6
- first_down: float32 [4608, 1024], P('tp', ('dp', 'ctx')), may hold values from -6 to 6
- second_norm1: float32 [1024], P(('dp', 'ctx')), may hold values from 1 to 100
- second_in: float32 [3, 1024, 1024], P(None, ('dp', 'ctx'), 'tp'), may hold values from 1 to 100
- second_conv: float32 [3, 1024], P(None, 'tp'), may hold values from 1 to 100
- second_out: float32 [1024, 1024], P('tp', ('dp', 'ctx')), may hold values from 1 to 100
- second_norm2: float32 [1024], P(('dp', 'ctx')), may hold values from 1 to 100
- second_gate_up: float32 [2, 1024, 4608], P(None, ('dp', 'ctx'), 'tp'), may hold values from 1 to 100
- second_down: float32 [4608, 1024], P('tp', ('dp', 'ctx')), may hold values from 1 to 100
Outputs:
- result: float32 [4, 256, 1024], P('dp', 'ctx')
- grad_tokens: float32 [4, 256, 1024], P('dp', 'ctx')
- grad_norm1: float32 [1024], P(('dp', 'ctx'))
- grad_in: float32 [3, 1024, 1024], P(None, ('dp', 'ctx'), 'tp')
- grad_conv: float32 [3, 1024], P(None, 'tp')
- grad_out: float32 [1024, 1024], P('tp', ('dp', 'ctx'))
- grad_norm2: float32 [1024], P(('dp', 'ctx'))
- grad_gate_up: float32 [2, 1024, 4608], P(None, ('dp', 'ctx'), 'tp')
- grad_down: float32 [4608, 1024], P('tp', ('dp', 'ctx'))
- new_norm1: float32 [1024], P(('dp', 'ctx'))
- new_in: float32 [3, 1024, 1024], P(None, ('dp', 'ctx'), 'tp')
- new_conv: float32 [3, 1024], P(None, 'tp')
- new_out: float32 [1024, 1024], P('tp', ('dp', 'ctx'))
- new_norm2: float32 [1024], P(('dp', 'ctx'))
- new_gate_up: float32 [2, 1024, 4608], P(None, ('dp', 'ctx'), 'tp')
- new_down: float32 [4608, 1024], P('tp', ('dp', 'ctx'))
- new_first_norm1: float32 [1024], P(('dp', 'ctx'))
- new_first_in: float32 [3, 1024, 1024], P(None, ('dp', 'ctx'), 'tp')
- new_first_conv: float32 [3, 1024], P(None, 'tp')
- new_first_out: float32 [1024, 1024], P('tp', ('dp', 'ctx'))
- new_first_norm2: float32 [1024], P(('dp', 'ctx'))
- new_first_gate_up: float32 [2, 1024, 4608], P(None, ('dp', 'ctx'), 'tp')
- new_first_down: float32 [4608, 1024], P('tp', ('dp', 'ctx'))
- new_second_norm1: float32 [1024], P(('dp', 'ctx'))
- new_second_in: float32 [3, 1024, 1024], P(None, ('dp', 'ctx'), 'tp')
- new_second_conv: float32 [3, 1024], P(None, 'tp')
- new_second_out: float32 [1024, 1024], P('tp', ('dp', 'ctx'))
- new_second_norm2: float32 [1024], P(('dp', 'ctx'))
- new_second_gate_up: float32 [2, 1024, 4608], P(None, ('dp', 'ctx'), 'tp')
- new_second_down: float32 [4608, 1024], P('tp', ('dp', 'ctx'))
Inputs may be any that keep to these rules, and one draw needn't show every extreme that they name: `doc_lengths`: each row holds 8 document lengths that add up to 256; the longest is exactly 64.
All inputs are finite; a program needn't handle non-finite values.
Results may differ from a plain program's by a relative error of at most 0.022.
Values may be sent and summed in bfloat16 or wider, within the bound.
No kernel may reach another device: no remote copies, remote signals or barrier semaphores. Data moves between devices by JAX's collectives and lax.ppermute only.
A program may use at most 128 MiB of HBM per device.

v0:
```python
import functools

import jax
import jax.numpy as jnp
from jax import lax
from jax.experimental import pallas as pl
from jax.experimental.layout import Layout, with_layout_constraint
from jax.experimental.pallas import tpu as pltpu
from jax.sharding import Mesh, PartitionSpec as P


STEP = 5


EPS_NORM = 1e-05
BETA_ONE = 0.9
BETA_TWO = 0.95
LEARN_RATE = 0.01
DECAY_RATE = 0.1
ADAM_EPS = 1e-08

DATA = ("dp", "ctx")
MODEL = ("lo", "hi")


bf16 = jnp.bfloat16
f32 = jnp.float32


def doc_masks(lengths_row, count):
    positions = jnp.arange(count, dtype=jnp.int32)
    starts = jnp.cumsum(lengths_row) - lengths_row
    inside = starts[None, :] <= positions[:, None]
    doc_start = jnp.max(jnp.where(inside, starts[None, :], jnp.int32(0)), axis=1)
    mask_one = (positions - 1 >= doc_start).astype(f32)[:, None]
    mask_two = (positions - 2 >= doc_start).astype(f32)[:, None]
    return (mask_one, mask_two)


def rms_scale(inputs):
    return lax.rsqrt(jnp.mean(inputs * inputs, axis=-1, keepdims=True) + EPS_NORM)


def norm_back(grad_normed, unit_rows, gain_full, scale_rows):
    scaled = grad_normed * gain_full
    return scale_rows * (scaled - unit_rows * jnp.mean(scaled * unit_rows, axis=-1, keepdims=True))


def adamw(param, grads, first, second, bias_one, bias_two):
    new_first = BETA_ONE * first + (1.0 - BETA_ONE) * grads
    new_second = BETA_TWO * second + (1.0 - BETA_TWO) * grads * grads
    update = (
        new_first / bias_one / (jnp.sqrt(new_second / bias_two) + ADAM_EPS) + DECAY_RATE * param
    )
    return (param - LEARN_RATE * update, new_first, new_second)


def exchange(blocks, axes):
    return lax.all_to_all(blocks, axes, 0, 0, tiled=True)


def shift(block, k):
    n = lax.axis_size("dp")
    return lax.ppermute(block, "dp", [(i, (i + k) % n) for i in range(n)])


def fetch_all(block):
    return [block] + [shift(block, k) for k in range(1, lax.axis_size("dp"))]


def send_each(blocks):
    return [blocks[0]] + [shift(blocks[k], k) for k in range(1, lax.axis_size("dp"))]


def by_distance(blocks):
    n = lax.axis_size("dp")
    at = lax.axis_index("dp")
    return [lax.dynamic_index_in_dim(blocks, (at + k) % n, 0, keepdims=False) for k in range(n)]


def by_member(items):
    n = lax.axis_size("dp")
    at = lax.axis_index("dp")
    stacked = jnp.stack(items)
    return jnp.stack(
        [lax.dynamic_index_in_dim(stacked, (at - q) % n, 0, keepdims=False) for q in range(n)]
    )


def swap(block, axis):
    return lax.ppermute(block, axis, [(0, 1), (1, 0)])


def gather(block, axis):
    if lax.axis_size(axis) == 2:
        other = swap(block, axis)
        first = lax.axis_index(axis) == 0
        return jnp.stack([jnp.where(first, block, other), jnp.where(first, other, block)])
    return lax.all_gather(block, axis)


def sum_scatter(blocks, axis):
    if lax.axis_size(axis) == 2:
        mine = lax.axis_index(axis)
        kept = lax.dynamic_index_in_dim(blocks, mine, 0, keepdims=False)
        given = lax.dynamic_index_in_dim(blocks, 1 - mine, 0, keepdims=False)
        return kept.astype(f32) + swap(given, axis).astype(f32)
    return jnp.sum(exchange(blocks, axis).astype(f32), axis=0)


def gather_last(block, axis):
    if lax.axis_size(axis) == 2:
        other = swap(block, axis)
        first = lax.axis_index(axis) == 0
        return jnp.concatenate(
            [jnp.where(first, block, other), jnp.where(first, other, block)], axis=-1
        )
    return lax.all_gather(block, axis, axis=block.ndim - 1, tiled=True)


def gather_features(block):
    return gather_last(gather_last(block, "hi"), "lo")


def row_major(block):
    return with_layout_constraint(block, Layout(major_to_minor=tuple(range(block.ndim))))


def dot_nt(left, right):
    return lax.dot_general(left, right, (((1,), (1,)), ((), ())), preferred_element_type=f32)


def dot_tn(left, right):
    return lax.dot_general(left, right, (((0,), (0,)), ((), ())), preferred_element_type=f32)


def ffn_body(n_dp, at, *refs):
    normed_own, normed_other, up_own, up_other = refs[:4]
    w_own = refs[4 : 4 + n_dp]
    w_other = refs[4 + n_dp : 4 + 2 * n_dp]
    kept_ffn, given_ffn, kept_grad, given_grad, kept_w, given_w = refs[4 + 2 * n_dp : 10 + 2 * n_dp]
    normed, upstream, weights, act, grad_gate, grad_up = refs[10 + 2 * n_dp :]
    f_three, lane = w_own[0].shape
    f_own = f_three // 3
    rows, half = normed_own.shape
    count = rows // n_dp
    n_hi = kept_ffn.shape[1]
    quarter = half // n_hi
    ctx_first = at[0] == 0
    lo_first = at[1] == 0

    def member(k):
        return lax.rem(at[2] + (n_dp - k), n_dp)

    def place(even, odd):
        for k in range(n_dp):
            left = pl.multiple_of(member(k) * (2 * lane), 2 * lane)
            weights[:, pl.ds(left, lane)] = even[k][...]
            weights[:, pl.ds(pl.multiple_of(left + lane, lane), lane)] = odd[k][...]

    @pl.when(ctx_first)
    def _():
        place(w_own, w_other)

    @pl.when(jnp.logical_not(ctx_first))
    def _():
        place(w_other, w_own)

    @pl.when(lo_first)
    def _():
        normed[:, :half] = normed_own[...]
        normed[:, half:] = normed_other[...]
        upstream[:, :half] = up_own[...]
        upstream[:, half:] = up_other[...]

    @pl.when(jnp.logical_not(lo_first))
    def _():
        normed[:, :half] = normed_other[...]
        normed[:, half:] = normed_own[...]
        upstream[:, :half] = up_other[...]
        upstream[:, half:] = up_own[...]

    tiles = 2
    tile = rows // tiles

    def step(i, carry):
        part = pl.ds(pl.multiple_of(i * tile, tile), tile)
        n_rows = normed[part, :]
        gate_pre = dot_nt(n_rows, weights[:f_own, :])
        up_pre = dot_nt(n_rows, weights[f_own : 2 * f_own, :])
        grad_act = dot_nt(upstream[part, :], weights[2 * f_own :, :])
        sig = 1.0 / (1.0 + jnp.exp(-gate_pre))
        gated = gate_pre * sig
        act[part, :] = (gated * up_pre).astype(bf16)
        grad_gate[part, :] = (grad_act * up_pre * sig * (1.0 + gate_pre * (1.0 - sig))).astype(bf16)
        grad_up[part, :] = (grad_act * gated).astype(bf16)

        def send(kept_out, given_out, values):
            kept = jnp.where(lo_first, values[:, :half], values[:, half:]).astype(bf16)
            given = jnp.where(lo_first, values[:, half:], values[:, :half]).astype(bf16)
            for j in range(n_dp // tiles):
                z = member(i * (n_dp // tiles) + j)
                for h in range(n_hi):
                    cut = (slice(j * count, (j + 1) * count), slice(h * quarter, (h + 1) * quarter))
                    kept_out[z, h] = kept[cut]
                    given_out[z, h] = given[cut]

        send(
            kept_ffn,
            given_ffn,
            jnp.dot(act[part, :], weights[2 * f_own :, :], preferred_element_type=f32),
        )
        send(
            kept_grad,
            given_grad,
            jnp.dot(grad_gate[part, :], weights[:f_own, :], preferred_element_type=f32)
            + jnp.dot(grad_up[part, :], weights[f_own : 2 * f_own, :], preferred_element_type=f32),
        )
        return carry

    lax.fori_loop(0, tiles, step, 0)

    for k, (left, right) in enumerate(((grad_gate, normed), (grad_up, normed), (act, upstream))):
        cut = slice(k * f_own, (k + 1) * f_own)
        for z in range(n_dp):
            away = lax.rem(z + n_dp - at[2], n_dp)
            pair = dot_tn(left[...], right[:, 2 * z * lane : (2 * z + 2) * lane])
            even = pair[:, :lane]
            odd = pair[:, lane:]
            kept_w[away, cut, :] = jnp.where(ctx_first, even, odd).astype(bf16)
            given_w[away, cut, :] = jnp.where(ctx_first, odd, even).astype(bf16)


def ffn_kernel(at, normed_own, normed_other, up_own, up_other, w_own, w_other, n_hi):
    n_dp = len(w_own)
    f_three, lane = w_own[0].shape
    rows, half = normed_own.shape
    parts = jax.ShapeDtypeStruct((n_dp, n_hi, rows // n_dp, half // n_hi), bf16)
    grads = jax.ShapeDtypeStruct((n_dp, f_three, lane), bf16)
    vmem = pl.BlockSpec(memory_space=pltpu.VMEM)
    hidden = pltpu.VMEM((rows, f_three // 3), bf16)
    return pl.pallas_call(
        functools.partial(ffn_body, n_dp),
        out_shape=(parts, parts, parts, parts, grads, grads),
        in_specs=[pl.BlockSpec(memory_space=pltpu.SMEM)] + [vmem] * (4 + 2 * n_dp),
        out_specs=[vmem] * 6,
        scratch_shapes=[
            pltpu.VMEM((rows, 2 * half), bf16),
            pltpu.VMEM((rows, 2 * half), bf16),
            pltpu.VMEM((f_three, 2 * n_dp * lane), bf16),
            hidden,
            hidden,
            hidden,
        ],
        compiler_params=pltpu.CompilerParams(vmem_limit_bytes=48 * 1024 * 1024),
        name="ffn",
    )(at, normed_own, normed_other, up_own, up_other, *w_own, *w_other)


def per_device(
    tokens,
    cotangent,
    doc_lengths,
    norm1_gain,
    in_weight,
    conv_weight,
    out_weight,
    norm2_gain,
    gate_up_weight,
    down_weight,
    first_norm1,
    first_in,
    first_conv,
    first_out,
    first_norm2,
    first_gate_up,
    first_down,
    second_norm1,
    second_in,
    second_conv,
    second_out,
    second_norm2,
    second_gate_up,
    second_down,
):
    n_dp = lax.axis_size("dp")
    n_ctx = lax.axis_size("ctx")
    n_hi = lax.axis_size("hi")
    n_lo = lax.axis_size("lo")
    n_tp = n_hi * n_lo
    n_data = n_dp * n_ctx
    at_ctx = lax.axis_index("ctx")
    at_lo = lax.axis_index("lo")

    rows = tokens.reshape(-1, tokens.shape[-1])
    upstream_f = cotangent.reshape(rows.shape)
    count, width = rows.shape
    length = count * n_ctx
    d_own = in_weight.shape[1]
    c_tp = in_weight.shape[2]
    c_own = c_tp // n_ctx
    f_tp = down_weight.shape[0]
    f_own = f_tp // n_dp
    half = width // n_lo
    quarter = width // n_tp

    mixer_own = jnp.concatenate([in_weight, out_weight.T[None]]).astype(bf16)
    mixer_own = mixer_own.reshape(4, d_own, n_ctx, c_own).transpose(2, 0, 1, 3)
    mixer_own = mixer_own.reshape(n_ctx, 4 * d_own, c_own)
    gains = jnp.concatenate([norm1_gain, norm2_gain]).astype(bf16)
    gains = jnp.pad(gains, (0, -gains.shape[0] % c_own)).reshape(-1, c_own)
    gains = jnp.broadcast_to(gains[None], (n_ctx, *gains.shape))
    mixer_own = jnp.concatenate([mixer_own, gains], axis=1)
    mixer_own = jnp.broadcast_to(mixer_own[None], (n_dp, *mixer_own.shape))
    mixer_all = exchange(mixer_own.reshape(n_data, -1, c_own), DATA)

    scale_one = rms_scale(rows)
    unit_one = rows * scale_one
    unit_seq = gather(unit_one.astype(bf16), "ctx").reshape(length, width)

    def half_rows(block):
        return lax.dynamic_slice_in_dim(block, at_lo * half, half, 1)

    ffn_own = jnp.concatenate(
        [gate_up_weight.astype(bf16).transpose(0, 2, 1), down_weight.astype(bf16)[None]]
    )
    ffn_own = ffn_own.reshape(3, n_dp, f_own, d_own).transpose(1, 0, 2, 3)
    ffn_own = by_distance(ffn_own.reshape(n_dp, 3 * f_own, d_own))
    up_own = half_rows(upstream_f.astype(bf16))
    mixer_all, ffn_own, up_own = lax.optimization_barrier((mixer_all, ffn_own, up_own))
    ffn_own = send_each(ffn_own)
    up_own = jnp.concatenate(fetch_all(up_own))

    w_mixer = mixer_all[:, : 4 * d_own].reshape(n_data, 4, d_own, c_own).transpose(1, 0, 2, 3)
    w_mixer = w_mixer.reshape(4, width, c_own)
    w_in = w_mixer[:3]
    w_out = w_mixer[3]
    gains_all = mixer_all[:, 4 * d_own :].reshape(n_data, -1).astype(f32)
    gain_one = gains_all[:, :d_own].reshape(width)
    gain_two = gains_all[:, d_own : 2 * d_own].reshape(width)
    normed_seq = (unit_seq.astype(f32) * gain_one).astype(bf16)

    mask_one, mask_two = doc_masks(doc_lengths[0], length + 2)
    taps = lax.dynamic_slice_in_dim(conv_weight, at_ctx * c_own, c_own, 1)
    projected = jnp.einsum("td,kdc->ktc", normed_seq, w_in, preferred_element_type=f32)
    gate_b = projected[0]
    gate_c = projected[1]
    values_x = projected[2]
    mixed_in = gate_b * values_x
    extended = jnp.pad(mixed_in, ((2, 0), (0, 0)))
    lag_one = extended[1 : length + 1] * mask_one[:length]
    lag_two = extended[:length] * mask_two[:length]
    conv_out = taps[0] * lag_two + taps[1] * lag_one + taps[2] * mixed_in
    gated_y = (gate_c * conv_out).astype(bf16)

    def mixer_sum(part):
        blocks = part.astype(bf16).reshape(n_ctx, count, n_tp, quarter).transpose(0, 2, 1, 3)
        blocks = exchange(blocks.reshape(n_ctx * n_tp, count, quarter), ("ctx", *MODEL))
        return jnp.sum(blocks.astype(f32), axis=0)

    mixer_part = dot_nt(gated_y, w_out)
    mixer_out = gather_features(mixer_sum(mixer_part).astype(bf16)).astype(f32)
    hidden_rows = rows + mixer_out
    scale_two = rms_scale(hidden_rows)
    unit_two = hidden_rows * scale_two
    normed_own = jnp.concatenate(fetch_all(half_rows((unit_two * gain_two).astype(bf16))))
    if n_ctx == 2 and n_lo == 2 and n_dp % 2 == 0 and d_own % 128 == 0 and f_own % 16 == 0:
        normed_other = swap(normed_own, "lo")
        up_other = swap(up_own, "lo")
        ffn_other = [swap(block, "ctx") for block in ffn_own]
        kept_ffn, given_ffn, kept_grad, given_grad, kept_w, given_w = ffn_kernel(
            jnp.stack([at_ctx, at_lo, lax.axis_index("dp")]),
            normed_own,
            normed_other,
            up_own,
            up_other,
            ffn_own,
            ffn_other,
            n_hi,
        )
        grad_part = (kept_grad.astype(f32) + swap(given_grad, "lo").astype(f32)).astype(bf16)
        ffn_part = (kept_ffn.astype(f32) + swap(given_ffn, "lo").astype(f32)).astype(bf16)
        grad_part = grad_part.reshape(n_dp * n_hi, count, quarter)
        ffn_part = ffn_part.reshape(n_dp * n_hi, count, quarter)
        grad_ffn = (kept_w.astype(f32) + swap(given_w, "ctx").astype(f32)).astype(bf16)
        grad_ffn = [grad_ffn[k] for k in range(n_dp)]
    else:
        by_order = by_member(list(normed_own.reshape(n_dp, count, half)))
        normed_two = gather_last(by_order.reshape(n_dp * count, half), "lo")
        by_order = by_member(list(up_own.reshape(n_dp, count, half)))
        upstream = gather_last(by_order.reshape(n_dp * count, half), "lo")
        w_ffn = gather(by_member(ffn_own), "ctx").reshape(n_ctx, n_dp, 3, f_own, d_own)
        w_ffn = w_ffn.transpose(2, 3, 1, 0, 4).reshape(3, f_own, width)
        w_gate_up = w_ffn[:2]
        w_down = w_ffn[2]
        gate_up = jnp.einsum("td,kfd->ktf", normed_two, w_gate_up, preferred_element_type=f32)
        gate_pre = gate_up[0]
        up_pre = gate_up[1]
        sig = jax.nn.sigmoid(gate_pre)
        activated = (gate_pre * sig * up_pre).astype(bf16)
        grad_act = dot_nt(upstream, w_down)
        grad_gate = (grad_act * up_pre * sig * (1.0 + gate_pre * (1.0 - sig))).astype(bf16)
        grad_up = (grad_act * gate_pre * sig).astype(bf16)
        both = jnp.stack([grad_gate, grad_up])

        def sum_pairs(part):
            part = part.astype(bf16).reshape(n_dp * count, n_lo, half).transpose(1, 0, 2)
            part = sum_scatter(part, "lo").astype(bf16)
            part = part.reshape(n_dp, count, n_hi, quarter).transpose(0, 2, 1, 3)
            return part.reshape(n_dp * n_hi, count, quarter)

        ffn_part = sum_pairs(jnp.dot(activated, w_down, preferred_element_type=f32))
        grad_part = sum_pairs(
            jnp.einsum("ktf,kfd->td", both, w_gate_up, preferred_element_type=f32)
        )
        grad_gate_up = jnp.einsum("ktf,td->kfd", both, normed_two, preferred_element_type=f32)
        grad_down = dot_tn(activated, upstream)
        grad_ffn = jnp.concatenate([grad_gate_up.astype(bf16), grad_down.astype(bf16)[None]])
        grad_ffn = grad_ffn.reshape(3 * f_own, n_dp, n_ctx, d_own).transpose(2, 1, 0, 3)
        grad_ffn = by_distance(sum_scatter(grad_ffn, "ctx").astype(bf16))

    grad_part = exchange(grad_part, ("dp", "hi"))
    grad_part, ffn_part, grad_ffn = lax.optimization_barrier((grad_part, ffn_part, grad_ffn))
    grad_ffn = send_each(grad_ffn)
    grad_part = jnp.sum(grad_part.astype(f32), axis=0).astype(bf16)
    grad_normed_two = gather_features(grad_part).astype(f32)

    ffn_part = exchange(ffn_part, ("dp", "hi"))

    grad_norm2 = jnp.sum(grad_normed_two * unit_two, axis=0)
    grad_hidden = upstream_f + norm_back(grad_normed_two, unit_two, gain_two, scale_two)
    grad_seq = gather(grad_hidden.astype(bf16), "ctx").reshape(length, width)

    grad_y = jnp.dot(grad_seq, w_out, preferred_element_type=f32)
    grad_out = dot_tn(grad_seq, gated_y)
    grad_c = grad_y * conv_out
    grad_conv_in = grad_y * gate_c
    grad_ext = jnp.pad(grad_conv_in, ((0, 2), (0, 0)))
    lead_one = (grad_ext * mask_one)[1 : length + 1]
    lead_two = (grad_ext * mask_two)[2:]
    grad_mixed = taps[2] * grad_conv_in + taps[1] * lead_one + taps[0] * lead_two
    grad_taps = jnp.stack(
        [
            jnp.sum(grad_conv_in * lag_two, axis=0),
            jnp.sum(grad_conv_in * lag_one, axis=0),
            jnp.sum(grad_conv_in * mixed_in, axis=0),
        ]
    )
    grad_gates = jnp.stack(
        [
            (grad_mixed * values_x).astype(bf16),
            grad_c.astype(bf16),
            (grad_mixed * gate_b).astype(bf16),
        ]
    )
    ffn_part, grad_ffn, _ = lax.optimization_barrier((ffn_part, grad_ffn, grad_gates))
    ffn_part = jnp.sum(ffn_part.astype(f32), axis=0).astype(bf16)
    result = hidden_rows + gather_features(ffn_part).astype(f32)
    grad_ffn = by_member(grad_ffn).reshape(n_dp, 3, f_own, d_own).transpose(1, 0, 2, 3)
    grad_ffn = grad_ffn.reshape(3, f_tp, d_own)
    owned_gate_up = row_major(grad_ffn[:2].transpose(0, 2, 1)).astype(f32)
    owned_down = grad_ffn[2].astype(f32)

    grad_in = jnp.einsum("td,ktc->kdc", normed_seq, grad_gates, preferred_element_type=f32)
    grad_mixer = jnp.concatenate([grad_in.astype(bf16), grad_out.astype(bf16)[None]])
    grad_mixer = grad_mixer.reshape(4, n_dp, n_ctx, d_own, c_own).transpose(1, 2, 0, 3, 4)
    grad_mixer = by_distance(grad_mixer.reshape(n_dp, n_ctx, 4 * d_own, c_own))
    grad_mixer = send_each(grad_mixer)
    grad_mixer = functools.reduce(jnp.add, [block.astype(f32) for block in grad_mixer])
    if n_ctx == 2:
        kept = lax.dynamic_index_in_dim(grad_mixer, at_ctx, 0, keepdims=False)
        given = lax.dynamic_index_in_dim(grad_mixer, 1 - at_ctx, 0, keepdims=False)
        other = swap(given.astype(bf16), "ctx").astype(f32)
        first = at_ctx == 0
        owned_mixer = jnp.stack([jnp.where(first, kept, other), jnp.where(first, other, kept)])
    else:
        owned_mixer = exchange(grad_mixer.astype(bf16), "ctx").astype(f32)
    owned_mixer = owned_mixer.reshape(n_ctx, 4, d_own, c_own).transpose(1, 2, 0, 3)
    owned_mixer = owned_mixer.reshape(4, d_own, c_tp)
    owned_in = owned_mixer[:3]
    owned_out = row_major(owned_mixer[3].T)

    normed_one_part = jnp.einsum("ktc,kdc->td", grad_gates, w_in, preferred_element_type=f32)
    grad_normed_one = gather_features(mixer_sum(normed_one_part).astype(bf16))
    grad_normed_one = grad_normed_one.astype(f32)
    grad_norm1 = jnp.sum(grad_normed_one * unit_one, axis=0)
    grad_tokens = grad_hidden + norm_back(grad_normed_one, unit_one, gain_one, scale_one)

    small = jnp.concatenate(
        [
            grad_norm1.reshape(n_data, d_own),
            grad_norm2.reshape(n_data, d_own),
            jnp.broadcast_to(grad_taps.reshape(1, -1), (n_data, grad_taps.size)),
        ],
        axis=1,
    )
    small = exchange(small, DATA)
    small = jnp.sum(small.reshape(n_dp, n_ctx, -1), axis=0)
    owned_norm1 = jnp.sum(small[:, :d_own], axis=0)
    owned_norm2 = jnp.sum(small[:, d_own : 2 * d_own], axis=0)
    grad_conv = small[:, 2 * d_own :].reshape(n_ctx, 3, c_own)
    grad_conv = grad_conv.transpose(1, 0, 2).reshape(3, c_tp)

    steps = jnp.float32(STEP)
    bias_one = 1.0 - jnp.power(jnp.float32(BETA_ONE), steps)
    bias_two = 1.0 - jnp.power(jnp.float32(BETA_TWO), steps)
    new_norm1, new_first_norm1, new_second_norm1 = adamw(
        norm1_gain, owned_norm1, first_norm1, second_norm1, bias_one, bias_two
    )
    new_in, new_first_in, new_second_in = adamw(
        in_weight, owned_in, first_in, second_in, bias_one, bias_two
    )
    new_conv, new_first_conv, new_second_conv = adamw(
        conv_weight, grad_conv, first_conv, second_conv, bias_one, bias_two
    )
    new_out, new_first_out, new_second_out = adamw(
        out_weight, owned_out, first_out, second_out, bias_one, bias_two
    )
    new_norm2, new_first_norm2, new_second_norm2 = adamw(
        norm2_gain, owned_norm2, first_norm2, second_norm2, bias_one, bias_two
    )
    new_gate_up, new_first_gate_up, new_second_gate_up = adamw(
        gate_up_weight, owned_gate_up, first_gate_up, second_gate_up, bias_one, bias_two
    )
    new_down, new_first_down, new_second_down = adamw(
        down_weight, owned_down, first_down, second_down, bias_one, bias_two
    )
    return (
        result.reshape(tokens.shape),
        grad_tokens.reshape(tokens.shape),
        owned_norm1,
        owned_in,
        grad_conv,
        owned_out,
        owned_norm2,
        owned_gate_up,
        owned_down,
        new_norm1,
        new_in,
        new_conv,
        new_out,
        new_norm2,
        new_gate_up,
        new_down,
        new_first_norm1,
        new_first_in,
        new_first_conv,
        new_first_out,
        new_first_norm2,
        new_first_gate_up,
        new_first_down,
        new_second_norm1,
        new_second_in,
        new_second_conv,
        new_second_out,
        new_second_norm2,
        new_second_gate_up,
        new_second_down,
    )


def solution(mesh):
    n_dp, n_ctx, n_tp = (mesh.shape[name] for name in ("dp", "ctx", "tp"))
    n_lo = 2 if n_tp % 2 == 0 else 1
    devices = mesh.devices.reshape(n_dp, n_ctx, n_tp // n_lo, n_lo)
    paired = Mesh(devices, ("dp", "ctx", "hi", "lo"))
    tp = ("hi", "lo")

    row = P("dp", "ctx", None)
    params = (
        P(DATA),
        P(None, DATA, tp),
        P(None, tp),
        P(tp, DATA),
        P(DATA),
        P(None, DATA, tp),
        P(tp, DATA),
    )

    return jax.shard_map(
        per_device,
        mesh=paired,
        in_specs=(row, row, P("dp", None), *params, *params, *params),
        out_specs=(row, row, *params, *params, *params, *params),
        check_vma=False,
    )
```

profile of v0, /device:TPU:0, one launch (start us, length us, event | category | flops | bytes accessed | tf_op | source)
XLA Modules:
  0.0 273.5 jit_solution(10027409015602214199)
XLA Ops:
  5.7 7.4 %all-to-all-start = ((bf16[8,514,128]{2,1,0:T(8,128)(2,1)}), bf16[8,514,128]{2,1,0:T(8,128)(2,1)}, u32[]{:S(2)}, u32[]{:S(2)}) async-start(bf16[8,514,128]{2,1,0:T(8,128)(2,1)} %bitcast.5), calls=%async_computation | async-start | bytes 2129920 | tf_op jit(solution)/shard_map/all_to_all | solution.py:59
  20.0 11.0 %collective-permute-done = bf16[128,1024]{1,0:T(8,128)(2,1)S(1)} collective-permute-done((bf16[128,1024]{1,0:T(8,128)(2,1)S(1)}, bf16[128,1024]{1,0:T(8,128)(2,1)S(1)}, u32[]{:S(2)}, u32[]{:S(2)}) %collective-permute-start) | collective-permute-done | bytes 262176 | tf_op jit(solution)/shard_map/ppermute | solution.py:91
  32.0 7.4 %all-to-all-done = bf16[8,514,128]{2,1,0:T(8,128)(2,1)} async-done(((bf16[8,514,128]{2,1,0:T(8,128)(2,1)}), bf16[8,514,128]{2,1,0:T(8,128)(2,1)}, u32[]{:S(2)}, u32[]{:S(2)}) %all-to-all-start) | async-done | bytes 1052704 | tf_op jit(solution)/shard_map/all_to_all | solution.py:59
  47.8 12.7 %all_to_all.34 = bf16[8,128,256]{2,1,0:T(8,128)(2,1)S(1)} all-to-all(bf16[8,128,256]{2,1,0:T(8,128)(2,1)S(1)} %bitcast.242), channel_id=1, replica_groups=mesh['dp'=4,'ctx'=2,'hi'=2,'lo'=2] {'ctx','lo','hi'}, dimensions={0} | all-to-all | bytes 1048576 | tf_op jit(solution)/shard_map/all_to_all | solution.py:59
  61.8 3.1 %collective-permute-done.1 = bf16[128,256]{1,0:T(8,128)(2,1)S(1)} collective-permute-done((bf16[128,256]{1,0:T(8,128)(2,1)S(1)}, bf16[128,256]{1,0:T(8,128)(2,1)S(1)}, u32[]{:S(2)}, u32[]{:S(2)}) %collective-permute-start.1) | collective-permute-done | bytes 65568 | tf_op jit(solution)/shard_map/ppermute | solution.py:91
  71.6 3.2 %collective-permute-done.8 = bf16[128,512]{1,0:T(8,128)(2,1)S(1)} collective-permute-done((bf16[128,512]{1,0:T(8,128)(2,1)S(1)}, bf16[128,512]{1,0:T(8,128)(2,1)S(1)}, u32[]{:S(2)}, u32[]{:S(2)}) %collective-permute-start.8) | collective-permute-done | bytes 131104 | tf_op jit(solution)/shard_map/ppermute | solution.py:64
  76.0 3.1 %collective-permute-done.9 = bf16[128,512]{1,0:T(8,128)(2,1)S(1)} collective-permute-done((bf16[128,512]{1,0:T(8,128)(2,1)S(1)}, bf16[128,512]{1,0:T(8,128)(2,1)S(1)}, u32[]{:S(2)}, u32[]{:S(2)}) %collective-permute-start.9) | collective-permute-done | bytes 131104 | tf_op jit(solution)/shard_map/ppermute | solution.py:64
  81.8 11.1 %collective-permute-done.4 = bf16[128,512]{1,0:T(8,128)(2,1)S(1)} collective-permute-done((bf16[128,512]{1,0:T(8,128)(2,1)S(1)}, bf16[128,512]{1,0:T(8,128)(2,1)S(1)}, u32[]{:S(2)}, u32[]{:S(2)}) %collective-permute-start.4) | collective-permute-done | bytes 131104 | tf_op jit(solution)/shard_map/ppermute | solution.py:64
  95.2 9.9 %collective-permute-done.12.refs_6_ = bf16[864,128]{1,0:T(8,128)(2,1)S(1)} collective-permute-done((bf16[864,128]{1,0:T(8,128)(2,1)S(1)}, bf16[864,128]{1,0:T(8,128)(2,1)S(1)}, u32[]{:S(2)}, u32[]{:S(2)}) %collective-permute-start.12) | collective-permute-done | bytes 221216 | tf_op jit(solution)/shard_map/ppermute | solution.py:64
  108.3 5.0 %collective-permute-done.15.refs_9_ = bf16[864,128]{1,0:T(8,128)(2,1)S(1)} collective-permute-done((bf16[864,128]{1,0:T(8,128)(2,1)S(1)}, bf16[864,128]{1,0:T(8,128)(2,1)S(1)}, u32[]{:S(2)}, u32[]{:S(2)}) %collective-permute-start.15) | collective-permute-done | bytes 221216 | tf_op jit(solution)/shard_map/ppermute | solution.py:91
  113.4 4.7 %collective-permute-done.16.refs_10_ = bf16[864,128]{1,0:T(8,128)(2,1)S(1)} collective-permute-done((bf16[864,128]{1,0:T(8,128)(2,1)S(1)}, bf16[864,128]{1,0:T(8,128)(2,1)S(1)}, u32[]{:S(2)}, u32[]{:S(2)}) %collective-permute-start.16) | collective-permute-done | bytes 221216 | tf_op jit(solution)/shard_map/ppermute | solution.py:91
  118.1 3.8 %collective-permute-done.17.refs_11_ = bf16[864,128]{1,0:T(8,128)(2,1)S(1)} collective-permute-done((bf16[864,128]{1,0:T(8,128)(2,1)S(1)}, bf16[864,128]{1,0:T(8,128)(2,1)S(1)}, u32[]{:S(2)}, u32[]{:S(2)}) %collective-permute-start.17) | collective-permute-done | bytes 221216 | tf_op jit(solution)/shard_map/ppermute | solution.py:91
  121.9 7.4 %ffn.1 = (bf16[4,2,128,256]{3,2,1,0:T(8,128)(2,1)S(1)}, bf16[4,2,128,256]{3,2,1,0:T(8,128)(2,1)S(1)}, bf16[4,2,128,256]{3,2,1,0:T(8,128)(2,1)S(1)}, bf16[4,2,128...) custom-call(s32[3]{0:T(128)S(1)} %pad_add_fusion.at, ...), custom_call_target="tpu_custom_call" | custom-call | tf_op jit(solution)/shard_map/ffn/pallas_call | solution.py:242
  132.2 6.6 %all-to-all-start.2 = ((bf16[8,128,256]{2,1,0:T(8,128)(2,1)}), bf16[8,128,256]{2,1,0:T(8,128)(2,1)}, u32[]{:S(2)}, u32[]{:S(2)}) async-start(bf16[8,128,256]{2,1,0:T(8,128)(2,1)} %bitcast.241), calls=%async_computation.2 | async-start | bytes 1048576 | tf_op jit(solution)/shard_map/all_to_all | solution.py:59
  140.9 10.8 %collective-permute-done.20 = bf16[4,864,128]{2,1,0:T(8,128)(2,1)} collective-permute-done((bf16[4,864,128]{2,1,0:T(8,128)(2,1)}, bf16[4,864,128]{2,1,0:T(8,128)(2,1)}, u32[]{:S(2)}, u32[]{:S(2)}) %collective-permute-start.20) | collective-permute-done | bytes 884768 | tf_op jit(solution)/shard_map/ppermute | solution.py:91
  156.4 3.1 %collective-permute-done.24 = bf16[128,256]{1,0:T(8,128)(2,1)S(1)} collective-permute-done((bf16[128,256]{1,0:T(8,128)(2,1)S(1)}, bf16[128,256]{1,0:T(8,128)(2,1)S(1)}, u32[]{:S(2)}, u32[]{:S(2)}) %collective-permute-start.24) | collective-permute-done | bytes 65568 | tf_op jit(solution)/shard_map/ppermute | solution.py:91
  162.3 7.6 %collective-permute-done.26 = bf16[128,1024]{1,0:T(8,128)(2,1)S(1)} collective-permute-done((bf16[128,1024]{1,0:T(8,128)(2,1)S(1)}, bf16[128,1024]{1,0:T(8,128)(2,1)S(1)}, u32[]{:S(2)}, u32[]{:S(2)}) %collective-permute-start.26) | collective-permute-done | bytes 262176 | tf_op jit(solution)/shard_map/ppermute | solution.py:91
  178.0 4.8 %collective-permute-start.33 = (bf16[2,512,128]{2,1,0:T(8,128)(2,1)}, bf16[2,512,128]{2,1,0:T(8,128)(2,1)}, u32[]{:S(2)}, u32[]{:S(2)}) collective-permute-start(bf16[2,512,128]{2,1,0:T(8,128)(2,1)} %get-tuple-element.232), channel_id=1, source_target_pairs={{0,24},{8,0},{16,8},{24,16},{1,25},{9,1},{17,9},{25,17},{2,26},{10... | collective-permute-start | bytes 786440 | tf_op jit(solution)/shard_map/ppermute | solution.py:64
  188.1 5.1 %all-to-all-start.3 = ((bf16[8,128,256]{2,1,0:T(8,128)(2,1)}), bf16[8,128,256]{2,1,0:T(8,128)(2,1)S(1)}, u32[]{:S(2)}, u32[]{:S(2)}) async-start(bf16[8,128,256]{2,1,0:T(8,128)(2,1)} %bitcast.43), calls=%async_computation.3 | async-start | bytes 1048576 | tf_op jit(solution)/shard_map/all_to_all | solution.py:59
  199.1 21.7 %collective-permute-done.32 = bf16[2,512,128]{2,1,0:T(8,128)(2,1)} collective-permute-done((bf16[2,512,128]{2,1,0:T(8,128)(2,1)}, bf16[2,512,128]{2,1,0:T(8,128)(2,1)}, u32[]{:S(2)}, u32[]{:S(2)}) %collective-permute-start.32) | collective-permute-done | bytes 262176 | tf_op jit(solution)/shard_map/ppermute | solution.py:64
  233.5 4.2 %all-to-all-start.4 = ((bf16[8,128,256]{2,1,0:T(8,128)(2,1)}), bf16[8,128,256]{2,1,0:T(8,128)(2,1)}, u32[]{:S(2)}, u32[]{:S(2)}) async-start(bf16[8,128,256]{2,1,0:T(8,128)(2,1)} %bitcast.60), calls=%async_computation.4 | async-start | bytes 1048576 | tf_op jit(solution)/shard_map/all_to_all | solution.py:59
  252.4 4.2 %multiply_subtract_fusion = (f32[2,128,1152]{2,1,0:T(8,128)}, f32[2,128,1152]{2,1,0:T(8,128)}, f32[2,128,1152]{2,1,0:T(8,128)}, f32[2,128,1152]{2,1,0:T(8,128)}) fusion(f32[2,128,1152]{2,1,0:T(8,128)S(1)} %copy-done.1, f32[2,128,1152]{2,1,0:T(8,128)} %param.46, f32[2,128,1152]{2,1,0:T(8,128)} %param.39, bf16[2,1152,128]{1,2,0:T(8,128)(2,1)S(1)} %copy.173), kind=kLoop, calls=%fused_computation.10 | loop fusion | flops 4718592 | bytes 8847360 | tf_op jit(solution)/shard_map/sub | solution.py:55
  261.5 3.3 %all-to-all-start.5 = ((f32[8,1,640]{2,1,0:T(1,128)}), f32[8,1,640]{2,1,0:T(1,128)S(1)}, u32[]{:S(2)}, u32[]{:S(2)}) async-start(f32[8,1,640]{2,1,0:T(1,128)} %all_to_all.26), calls=%async_computation.5 | async-start | bytes 40960 | tf_op jit(solution)/shard_map/all_to_all | solution.py:59
  266.4 5.0 %all-to-all-done.5 = f32[8,1,640]{2,1,0:T(1,128)S(1)} async-done(((f32[8,1,640]{2,1,0:T(1,128)}), f32[8,1,640]{2,1,0:T(1,128)S(1)}, u32[]{:S(2)}, u32[]{:S(2)}) %all-to-all-start.5) | async-done | bytes 20512 | tf_op jit(solution)/shard_map/all_to_all | solution.py:59
  (345 shorter events, 105.0 us)
Async XLA Ops:
  5.7 33.7 %all-to-all-start = ((bf16[8,514,128]{2,1,0:T(8,128)(2,1)}), bf16[8,514,128]{2,1,0:T(8,128)(2,1)}, u32[]{:S(2)}, u32[]{:S(2)}) async-start(bf16[8,514,128]{2,1,0:T(8,128)(2,1)} %bitcast.5), calls=%async_computation | async-start | bytes 2129920 | tf_op jit(solution)/shard_map/all_to_all | solution.py:59
  13.4 17.6 %collective-permute-start = (bf16[128,1024]{1,0:T(8,128)(2,1)S(1)}, bf16[128,1024]{1,0:T(8,128)(2,1)S(1)}, u32[]{:S(2)}, u32[]{:S(2)}) collective-permute-start(bf16[128,1024]{1,0:T(8,128)(2,1)S(1)} %fusion.19), channel_id=1, source_target_pairs={{0,4},{4,0},{1,5},{5,1},{2,6},{6,2},{3,7},{7,3},{8,12},{12,8},{9,1... | collective-permute-start | bytes 786440 | tf_op jit(solution)/shard_map/ppermute | solution.py:91
  65.1 13.9 %collective-permute-start.9 = (bf16[128,512]{1,0:T(8,128)(2,1)S(1)}, bf16[128,512]{1,0:T(8,128)(2,1)S(1)}, u32[]{:S(2)}, u32[]{:S(2)}) collective-permute-start(bf16[128,512]{1,0:T(8,128)(2,1)S(1)} %copy-done.34), channel_id=1, source_target_pairs={{0,24},{8,0},{16,8},{24,16},{1,25},{9,1},{17,9},{25,17},{2,26},{10... | collective-permute-start | bytes 393224 | tf_op jit(solution)/shard_map/ppermute | solution.py:64
  66.8 27.7 %collective-permute-start.11 = (bf16[864,128]{1,0:T(8,128)(2,1)S(1)}, bf16[864,128]{1,0:T(8,128)(2,1)S(1)}, u32[]{:S(2)}, u32[]{:S(2)}) collective-permute-start(bf16[864,128]{1,0:T(8,128)(2,1)S(1)} %copy-done.43), channel_id=1, source_target_pairs={{0,8},{8,16},{16,24},{24,0},{1,9},{9,17},{17,25},{25,1},{2,10},{10... | collective-permute-start | bytes 663560 | tf_op jit(solution)/shard_map/ppermute | solution.py:64
  69.9 12.0 %collective-permute-start.5 = (bf16[128,512]{1,0:T(8,128)(2,1)S(1)}, bf16[128,512]{1,0:T(8,128)(2,1)S(1)}, u32[]{:S(2)}, u32[]{:S(2)}) collective-permute-start(bf16[128,512]{1,0:T(8,128)(2,1)S(1)} %fusion.22), channel_id=1, source_target_pairs={{0,24},{8,0},{16,8},{24,16},{1,25},{9,1},{17,9},{25,17},{2,26},{10... | collective-permute-start | bytes 393224 | tf_op jit(solution)/shard_map/ppermute | solution.py:64
  71.4 21.6 %collective-permute-start.4 = (bf16[128,512]{1,0:T(8,128)(2,1)S(1)}, bf16[128,512]{1,0:T(8,128)(2,1)S(1)}, u32[]{:S(2)}, u32[]{:S(2)}) collective-permute-start(bf16[128,512]{1,0:T(8,128)(2,1)S(1)} %fusion.22), channel_id=1, source_target_pairs={{0,16},{8,24},{16,0},{24,8},{1,17},{9,25},{17,1},{25,9},{2,18},{10... | collective-permute-start | bytes 393224 | tf_op jit(solution)/shard_map/ppermute | solution.py:64
  74.8 18.2 %collective-permute-start.3 = (bf16[128,512]{1,0:T(8,128)(2,1)S(1)}, bf16[128,512]{1,0:T(8,128)(2,1)S(1)}, u32[]{:S(2)}, u32[]{:S(2)}) collective-permute-start(bf16[128,512]{1,0:T(8,128)(2,1)S(1)} %fusion.22), channel_id=1, source_target_pairs={{0,8},{8,16},{16,24},{24,0},{1,9},{9,17},{17,25},{25,1},{2,10},{10... | collective-permute-start | bytes 393224 | tf_op jit(solution)/shard_map/ppermute | solution.py:64
  79.0 42.8 %collective-permute-start.10 = (bf16[512,512]{1,0:T(8,128)(2,1)S(1)}, bf16[512,512]{1,0:T(8,128)(2,1)S(1)}, u32[]{:S(2)}, u32[]{:S(2)}) collective-permute-start(bf16[512,512]{1,0:T(8,128)(2,1)S(1)} %constant_dynamic-update-slice_fusion.refs_2_), channel_id=1, source_target_pairs={{0,1},{1,0},{2,3},{3,2},{4,5},{5,4},{6,7},{7,6},{8,9},{9,8},{10,11... | collective-permute-start | bytes 1572872 | tf_op jit(solution)/shard_map/ppermute | solution.py:91
  93.0 28.8 %collective-permute-start.6 = (bf16[512,512]{1,0:T(8,128)(2,1)S(1)}, bf16[512,512]{1,0:T(8,128)(2,1)S(1)}, u32[]{:S(2)}, u32[]{:S(2)}) collective-permute-start(bf16[512,512]{1,0:T(8,128)(2,1)S(1)} %pad_maximum_fusion.3.refs_0_), channel_id=1, source_target_pairs={{0,1},{1,0},{2,3},{3,2},{4,5},{5,4},{6,7},{7,6},{8,9},{9,8},{10,11... | collective-permute-start | bytes 1572872 | tf_op jit(solution)/shard_map/ppermute | solution.py:91
  93.2 11.9 %collective-permute-start.12 = (bf16[864,128]{1,0:T(8,128)(2,1)S(1)}, bf16[864,128]{1,0:T(8,128)(2,1)S(1)}, u32[]{:S(2)}, u32[]{:S(2)}) collective-permute-start(bf16[864,128]{1,0:T(8,128)(2,1)S(1)} %copy-done.42), channel_id=1, source_target_pairs={{0,16},{8,24},{16,0},{24,8},{1,17},{9,25},{17,1},{25,9},{2,18},{10... | collective-permute-start | bytes 663560 | tf_op jit(solution)/shard_map/ppermute | solution.py:64
  94.0 12.2 %collective-permute-start.13 = (bf16[864,128]{1,0:T(8,128)(2,1)S(1)}, bf16[864,128]{1,0:T(8,128)(2,1)S(1)}, u32[]{:S(2)}, u32[]{:S(2)}) collective-permute-start(bf16[864,128]{1,0:T(8,128)(2,1)S(1)} %copy-done.41), channel_id=1, source_target_pairs={{0,24},{8,0},{16,8},{24,16},{1,25},{9,1},{17,9},{25,17},{2,26},{10... | collective-permute-start | bytes 663560 | tf_op jit(solution)/shard_map/ppermute | solution.py:64
  94.5 12.6 %collective-permute-start.14 = (bf16[864,128]{1,0:T(8,128)(2,1)S(1)}, bf16[864,128]{1,0:T(8,128)(2,1)S(1)}, u32[]{:S(2)}, u32[]{:S(2)}) collective-permute-start(bf16[864,128]{1,0:T(8,128)(2,1)S(1)} %get-tuple-element.55.refs_4_), channel_id=1, source_target_pairs={{0,4},{4,0},{1,5},{5,1},{2,6},{6,2},{3,7},{7,3},{8,12},{12,8},{9,1... | collective-permute-start | bytes 663560 | tf_op jit(solution)/shard_map/ppermute | solution.py:91
  106.2 11.9 %collective-permute-start.16 = (bf16[864,128]{1,0:T(8,128)(2,1)S(1)}, bf16[864,128]{1,0:T(8,128)(2,1)S(1)}, u32[]{:S(2)}, u32[]{:S(2)}) collective-permute-start(bf16[864,128]{1,0:T(8,128)(2,1)S(1)} %collective-permute-done.12.refs_6_), channel_id=1, source_target_pairs={{0,4},{4,0},{1,5},{5,1},{2,6},{6,2},{3,7},{7,3},{8,12},{12,8},{9,1... | collective-permute-start | bytes 663560 | tf_op jit(solution)/shard_map/ppermute | solution.py:91
  107.1 14.8 %collective-permute-start.17 = (bf16[864,128]{1,0:T(8,128)(2,1)S(1)}, bf16[864,128]{1,0:T(8,128)(2,1)S(1)}, u32[]{:S(2)}, u32[]{:S(2)}) collective-permute-start(bf16[864,128]{1,0:T(8,128)(2,1)S(1)} %collective-permute-done.13.refs_7_), channel_id=1, source_target_pairs={{0,4},{4,0},{1,5},{5,1},{2,6},{6,2},{3,7},{7,3},{8,12},{12,8},{9,1... | collective-permute-start | bytes 663560 | tf_op jit(solution)/shard_map/ppermute | solution.py:91
  129.3 22.4 %collective-permute-start.20 = (bf16[4,864,128]{2,1,0:T(8,128)(2,1)}, bf16[4,864,128]{2,1,0:T(8,128)(2,1)}, u32[]{:S(2)}, u32[]{:S(2)}) collective-permute-start(bf16[4,864,128]{2,1,0:T(8,128)(2,1)} %get-tuple-element.64), channel_id=1, source_target_pairs={{0,4},{4,0},{1,5},{5,1},{2,6},{6,2},{3,7},{7,3},{8,12},{12,8},{9,1... | collective-permute-start | bytes 2654216 | tf_op jit(solution)/shard_map/ppermute | solution.py:91
  132.2 21.9 %all-to-all-start.2 = ((bf16[8,128,256]{2,1,0:T(8,128)(2,1)}), bf16[8,128,256]{2,1,0:T(8,128)(2,1)}, u32[]{:S(2)}, u32[]{:S(2)}) async-start(bf16[8,128,256]{2,1,0:T(8,128)(2,1)} %bitcast.241), calls=%async_computation.2 | async-start | bytes 1048576 | tf_op jit(solution)/shard_map/all_to_all | solution.py:59
  178.0 19.7 %collective-permute-start.33 = (bf16[2,512,128]{2,1,0:T(8,128)(2,1)}, bf16[2,512,128]{2,1,0:T(8,128)(2,1)}, u32[]{:S(2)}, u32[]{:S(2)}) collective-permute-start(bf16[2,512,128]{2,1,0:T(8,128)(2,1)} %get-tuple-element.232), channel_id=1, source_target_pairs={{0,24},{8,0},{16,8},{24,16},{1,25},{9,1},{17,9},{25,17},{2,26},{10... | collective-permute-start | bytes 786440 | tf_op jit(solution)/shard_map/ppermute | solution.py:64
  182.8 38.0 %collective-permute-start.32 = (bf16[2,512,128]{2,1,0:T(8,128)(2,1)}, bf16[2,512,128]{2,1,0:T(8,128)(2,1)}, u32[]{:S(2)}, u32[]{:S(2)}) collective-permute-start(bf16[2,512,128]{2,1,0:T(8,128)(2,1)} %get-tuple-element.233), channel_id=1, source_target_pairs={{0,16},{8,24},{16,0},{24,8},{1,17},{9,25},{17,1},{25,9},{2,18},{10... | collective-permute-start | bytes 786440 | tf_op jit(solution)/shard_map/ppermute | solution.py:64
  182.8 38.0 %collective-permute-start.31 = (bf16[2,512,128]{2,1,0:T(8,128)(2,1)}, bf16[2,512,128]{2,1,0:T(8,128)(2,1)}, u32[]{:S(2)}, u32[]{:S(2)}) collective-permute-start(bf16[2,512,128]{2,1,0:T(8,128)(2,1)} %get-tuple-element.231), channel_id=1, source_target_pairs={{0,8},{8,16},{16,24},{24,0},{1,9},{9,17},{17,25},{25,1},{2,10},{10... | collective-permute-start | bytes 786440 | tf_op jit(solution)/shard_map/ppermute | solution.py:64
  188.1 45.4 %all-to-all-start.3 = ((bf16[8,128,256]{2,1,0:T(8,128)(2,1)}), bf16[8,128,256]{2,1,0:T(8,128)(2,1)S(1)}, u32[]{:S(2)}, u32[]{:S(2)}) async-start(bf16[8,128,256]{2,1,0:T(8,128)(2,1)} %bitcast.43), calls=%async_computation.3 | async-start | bytes 1048576 | tf_op jit(solution)/shard_map/all_to_all | solution.py:59
  193.2 51.9 %collective-permute-start.21 = (bf16[864,128]{1,0:T(8,128)(2,1)}, bf16[864,128]{1,0:T(8,128)(2,1)}, u32[]{:S(2)}, u32[]{:S(2)}) collective-permute-start(bf16[864,128]{1,0:T(8,128)(2,1)} %get-tuple-element.67), channel_id=1, source_target_pairs={{0,8},{8,16},{16,24},{24,0},{1,9},{9,17},{17,25},{25,1},{2,10},{10... | collective-permute-start | bytes 663560 | tf_op jit(solution)/shard_map/ppermute | solution.py:64
  195.3 49.8 %collective-permute-start.22 = (bf16[864,128]{1,0:T(8,128)(2,1)}, bf16[864,128]{1,0:T(8,128)(2,1)}, u32[]{:S(2)}, u32[]{:S(2)}) collective-permute-start(bf16[864,128]{1,0:T(8,128)(2,1)} %get-tuple-element.68), channel_id=1, source_target_pairs={{0,16},{8,24},{16,0},{24,8},{1,17},{9,25},{17,1},{25,9},{2,18},{10... | collective-permute-start | bytes 663560 | tf_op jit(solution)/shard_map/ppermute | solution.py:64
  197.7 47.4 %collective-permute-start.23 = (bf16[864,128]{1,0:T(8,128)(2,1)}, bf16[864,128]{1,0:T(8,128)(2,1)}, u32[]{:S(2)}, u32[]{:S(2)}) collective-permute-start(bf16[864,128]{1,0:T(8,128)(2,1)} %get-tuple-element.69), channel_id=1, source_target_pairs={{0,24},{8,0},{16,8},{24,16},{1,25},{9,1},{17,9},{25,17},{2,26},{10... | collective-permute-start | bytes 663560 | tf_op jit(solution)/shard_map/ppermute | solution.py:64
  233.5 14.0 %all-to-all-start.4 = ((bf16[8,128,256]{2,1,0:T(8,128)(2,1)}), bf16[8,128,256]{2,1,0:T(8,128)(2,1)}, u32[]{:S(2)}, u32[]{:S(2)}) async-start(bf16[8,128,256]{2,1,0:T(8,128)(2,1)} %bitcast.60), calls=%async_computation.4 | async-start | bytes 1048576 | tf_op jit(solution)/shard_map/all_to_all | solution.py:59
  (92 other events, 678.4 us)
where the time goes:
time: 275 us; the launch traced here: 273 us
  waiting for transfers between devices  118 us (43%)
  starting transfers between devices  57.5 us (21%)
  other arithmetic  37.1 us (13%)
  local copies, waits for them, and re-layouts  34.1 us (12%)
  blocking collectives  12.7 us (5%)
  Pallas kernels  7.44 us (3%)
  matrix products  4.37 us (2%)
    ppermute x15, waiting for transfers between devices, shift(): return lax.ppermute(block, 'dp', [(i, (i + k) % n) for i in range(n)])  54 us
    ppermute x20, waiting for transfers between devices, swap(): return lax.ppermute(block, axis, [(0, 1), (1, 0)])  51.7 us
    all_to_all x5, starting transfers between devices, exchange(): return lax.all_to_all(blocks, axes, 0, 0, tiled=True)  26.7 us
    ppermute x15, starting transfers between devices, shift(): return lax.ppermute(block, 'dp', [(i, (i + k) % n) for i in range(n)])  17.6 us
    unnamed x164, local copies, waits for them, and re-layouts  14.3 us
    ppermute x20, starting transfers between devices, swap(): return lax.ppermute(block, axis, [(0, 1), (1, 0)])  13.3 us
    all_to_all x1, blocking collectives, exchange(): return lax.all_to_all(blocks, axes, 0, 0, tiled=True)  12.7 us
    all_to_all x5, waiting for transfers between devices, exchange(): return lax.all_to_all(blocks, axes, 0, 0, tiled=True)  12.4 us
  transfers between devices with their start and end apart: 40, of which 21 were waited for; matrix products, arithmetic and copies ran while one was open for 17% of the time, Pallas kernels for 0%

commit v1 on v0

--- a/solution.py
+++ b/solution.py
@@ -119,7 +119,8 @@
 
 
 def gather_features(block):
-    return gather_last(gather_last(block, "hi"), "lo")
+    block = gather_last(block, "hi")
+    return gather_last(block, "lo")
 
 
 def row_major(block):
@@ -326,10 +327,13 @@
     )
     ffn_own = ffn_own.reshape(3, n_dp, f_own, d_own).transpose(1, 0, 2, 3)
     ffn_own = by_distance(ffn_own.reshape(n_dp, 3 * f_own, d_own))
-    up_own = half_rows(upstream_f.astype(bf16))
+    own_other = swap(ffn_own[0], "ctx") if n_ctx == 2 else None
+    at_quarter = at_lo * n_hi + lax.axis_index("hi")
+    up_own = lax.dynamic_slice_in_dim(upstream_f.astype(bf16), at_quarter * quarter, quarter, 1)
     mixer_all, ffn_own, up_own = lax.optimization_barrier((mixer_all, ffn_own, up_own))
     ffn_own = send_each(ffn_own)
     up_own = jnp.concatenate(fetch_all(up_own))
+    up_own = gather_last(up_own, "hi")
 
     w_mixer = mixer_all[:, : 4 * d_own].reshape(n_data, 4, d_own, c_own).transpose(1, 0, 2, 3)
     w_mixer = w_mixer.reshape(4, width, c_own)
@@ -367,7 +371,7 @@
     if n_ctx == 2 and n_lo == 2 and n_dp % 2 == 0 and d_own % 128 == 0 and f_own % 16 == 0:
         normed_other = swap(normed_own, "lo")
         up_other = swap(up_own, "lo")
-        ffn_other = [swap(block, "ctx") for block in ffn_own]
+        ffn_other = [own_other] + [swap(block, "ctx") for block in ffn_own[1:]]
         kept_ffn, given_ffn, kept_grad, given_grad, kept_w, given_w = ffn_kernel(
             jnp.stack([at_ctx, at_lo, lax.axis_index("dp")]),
             normed_own,
@@ -380,8 +384,6 @@
         )
         grad_part = (kept_grad.astype(f32) + swap(given_grad, "lo").astype(f32)).astype(bf16)
         ffn_part = (kept_ffn.astype(f32) + swap(given_ffn, "lo").astype(f32)).astype(bf16)
-        grad_part = grad_part.reshape(n_dp * n_hi, count, quarter)
-        ffn_part = ffn_part.reshape(n_dp * n_hi, count, quarter)
         grad_ffn = (kept_w.astype(f32) + swap(given_w, "ctx").astype(f32)).astype(bf16)
         grad_ffn = [grad_ffn[k] for k in range(n_dp)]
     else:
@@ -406,8 +408,7 @@
         def sum_pairs(part):
             part = part.astype(bf16).reshape(n_dp * count, n_lo, half).transpose(1, 0, 2)
             part = sum_scatter(part, "lo").astype(bf16)
-            part = part.reshape(n_dp, count, n_hi, quarter).transpose(0, 2, 1, 3)
-            return part.reshape(n_dp * n_hi, count, quarter)
+            return part.reshape(n_dp, count, n_hi, quarter).transpose(0, 2, 1, 3)
 
         ffn_part = sum_pairs(jnp.dot(activated, w_down, preferred_element_type=f32))
         grad_part = sum_pairs(
@@ -419,13 +420,15 @@
         grad_ffn = grad_ffn.reshape(3 * f_own, n_dp, n_ctx, d_own).transpose(2, 1, 0, 3)
         grad_ffn = by_distance(sum_scatter(grad_ffn, "ctx").astype(bf16))
 
-    grad_part = exchange(grad_part, ("dp", "hi"))
+    grad_part = exchange(grad_part.reshape(n_dp * n_hi, count, quarter), ("dp", "hi"))
     grad_part, ffn_part, grad_ffn = lax.optimization_barrier((grad_part, ffn_part, grad_ffn))
     grad_ffn = send_each(grad_ffn)
     grad_part = jnp.sum(grad_part.astype(f32), axis=0).astype(bf16)
     grad_normed_two = gather_features(grad_part).astype(f32)
 
-    ffn_part = exchange(ffn_part, ("dp", "hi"))
+    ffn_part = sum_scatter(ffn_part.transpose(1, 0, 2, 3), "hi").astype(bf16)
+    ffn_part = by_distance(ffn_part)
+    ffn_part = send_each(ffn_part)
 
     grad_norm2 = jnp.sum(grad_normed_two * unit_two, axis=0)
     grad_hidden = upstream_f + norm_back(grad_normed_two, unit_two, gain_two, scale_two)
@@ -454,7 +457,7 @@
         ]
     )
     ffn_part, grad_ffn, _ = lax.optimization_barrier((ffn_part, grad_ffn, grad_gates))
-    ffn_part = jnp.sum(ffn_part.astype(f32), axis=0).astype(bf16)
+    ffn_part = functools.reduce(jnp.add, [part.astype(f32) for part in ffn_part]).astype(bf16)
     result = hidden_rows + gather_features(ffn_part).astype(f32)
     grad_ffn = by_member(grad_ffn).reshape(n_dp, 3, f_own, d_own).transpose(1, 0, 2, 3)
     grad_ffn = grad_ffn.reshape(3, f_tp, d_own)
@@ -477,7 +480,7 @@
         owned_mixer = exchange(grad_mixer.astype(bf16), "ctx").astype(f32)
     owned_mixer = owned_mixer.reshape(n_ctx, 4, d_own, c_own).transpose(1, 2, 0, 3)
     owned_mixer = owned_mixer.reshape(4, d_own, c_tp)
-    owned_in = owned_mixer[:3]
+    owned_in = row_major(owned_mixer[:3])
     owned_out = row_major(owned_mixer[3].T)
 
     normed_one_part = jnp.einsum("ktc,kdc->td", grad_gates, w_in, preferred_element_type=f32)

time: 275 us -> 255 us (0.927)
  starting transfers between devices: 57.5 us -> 72.7 us
  blocking collectives: 12.7 us -> 0 us
  local copies, waits for them, and re-layouts: 34.1 us -> 21.9 us
  waiting for transfers between devices: 118 us -> 110 us
    all_to_all x1 -> x0, blocking collectives: 12.7 us -> none  [exchange(): return lax.all_to_all(blocks, axes, 0, 0, tiled=True)]
    ppermute x15 -> x18, starting transfers between devices: 17.6 us -> 28.6 us  [shift(): return lax.ppermute(block, 'dp', [(i, (i + k) % n) for i in range(n)])]
    unnamed x164 -> x143, local copies, waits for them, and re-layouts: 14.3 us -> 4.63 us
    ppermute x20 -> x22, waiting for transfers between devices: 51.7 us -> 43.5 us  [swap(): return lax.ppermute(block, axis, [(0, 1), (1, 0)])]
    all_to_all x5, waiting for transfers between devices: 12.4 us -> 16.9 us  [exchange(): return lax.all_to_all(blocks, axes, 0, 0, tiled=True)]
    ppermute x15 -> x18, waiting for transfers between devices: 54 us -> 49.5 us  [shift(): return lax.ppermute(block, 'dp', [(i, (i + k) % n) for i in range(n)])]
    ppermute x20 -> x22, starting transfers between devices: 13.3 us -> 16.6 us  [swap(): return lax.ppermute(block, axis, [(0, 1), (1, 0)])]
  transfers between devices with their start and end apart: 40 -> 45, of which waited for: 21 -> 22; matrix products, arithmetic and copies ran while one was open for 17% -> 17% of each run, Pallas kernels for 0% -> 0%
where the time goes in v1:
time: 255 us; the launch traced here: 254 us
  waiting for transfers between devices  110 us (43%)
  starting transfers between devices  72.7 us (29%)
  other arithmetic  35.8 us (14%)
  local copies, waits for them, and re-layouts  21.9 us (9%)
  Pallas kernels  7.44 us (3%)
  matrix products  3.84 us (2%)
    ppermute x18, waiting for transfers between devices, shift(): return lax.ppermute(block, 'dp', [(i, (i + k) % n) for i in range(n)])  49.5 us
    ppermute x22, waiting for transfers between devices, swap(): return lax.ppermute(block, axis, [(0, 1), (1, 0)])  43.5 us
    ppermute x18, starting transfers between devices, shift(): return lax.ppermute(block, 'dp', [(i, (i + k) % n) for i in range(n)])  28.6 us
    all_to_all x5, starting transfers between devices, exchange(): return lax.all_to_all(blocks, axes, 0, 0, tiled=True)  27.5 us
    all_to_all x5, waiting for transfers between devices, exchange(): return lax.all_to_all(blocks, axes, 0, 0, tiled=True)  16.9 us
    ppermute x22, starting transfers between devices, swap(): return lax.ppermute(block, axis, [(0, 1), (1, 0)])  16.6 us
    sub x7, other arithmetic, adamw(): return (param - LEARN_RATE * update, new_first, new_second)  10.6 us
    pallas_call x1, Pallas kernels, ffn_kernel(): pl.pallas_call(functools.partial(ffn_body, n_dp), out_shape=(parts, parts...  7.44 us
  transfers between devices with their start and end apart: 45, of which 22 were waited for; matrix products, arithmetic and copies ran while one was open for 17% of the time, Pallas kernels for 0%

profile of v1, /device:TPU:0, one launch (start us, length us, event | category | flops | bytes accessed | tf_op | source)
XLA Modules:
  0.0 253.8 jit_solution(9691545032387103964)
XLA Ops:
  5.7 7.4 %all-to-all-start = ((bf16[8,514,128]{2,1,0:T(8,128)(2,1)}), bf16[8,514,128]{2,1,0:T(8,128)(2,1)S(1)}, u32[]{:S(2)}, u32[]{:S(2)}) async-start(bf16[8,514,128]{2,1,0:T(8,128)(2,1)} %bitcast.5), calls=%async_computation | async-start | bytes 2129920 | tf_op jit(solution)/shard_map/all_to_all | solution.py:59
  22.1 9.0 %collective-permute-done = bf16[128,1024]{1,0:T(8,128)(2,1)} collective-permute-done((bf16[128,1024]{1,0:T(8,128)(2,1)S(1)}, bf16[128,1024]{1,0:T(8,128)(2,1)}, u32[]{:S(2)}, u32[]{:S(2)}) %collective-permute-start) | collective-permute-done | bytes 262176 | tf_op jit(solution)/shard_map/ppermute | solution.py:91
  32.9 6.3 %all-to-all-done = bf16[8,514,128]{2,1,0:T(8,128)(2,1)S(1)} async-done(((bf16[8,514,128]{2,1,0:T(8,128)(2,1)}), bf16[8,514,128]{2,1,0:T(8,128)(2,1)S(1)}, u32[]{:S(2)}, u32[]{:S(2)}) %all-to-all-start) | async-done | bytes 1052704 | tf_op jit(solution)/shard_map/all_to_all | solution.py:59
  45.8 3.6 %all-to-all-start.1 = ((bf16[8,128,256]{2,1,0:T(8,128)(2,1)}), bf16[8,128,256]{2,1,0:T(8,128)(2,1)S(1)}, u32[]{:S(2)}, u32[]{:S(2)}) async-start(bf16[8,128,256]{2,1,0:T(8,128)(2,1)} %bitcast.35), calls=%async_computation.1 | async-start | bytes 1048576 | tf_op jit(solution)/shard_map/all_to_all | solution.py:59
  55.3 3.5 %all-to-all-done.1 = bf16[8,128,256]{2,1,0:T(8,128)(2,1)S(1)} async-done(((bf16[8,128,256]{2,1,0:T(8,128)(2,1)}), bf16[8,128,256]{2,1,0:T(8,128)(2,1)S(1)}, u32[]{:S(2)}, u32[]{:S(2)}) %all-to-all-start.1) | async-done | bytes 524320 | tf_op jit(solution)/shard_map/all_to_all | solution.py:59
  67.8 4.3 %collective-permute-done.10 = bf16[512,256]{1,0:T(8,128)(2,1)S(1)} collective-permute-done((bf16[512,256]{1,0:T(8,128)(2,1)S(1)}, bf16[512,256]{1,0:T(8,128)(2,1)S(1)}, u32[]{:S(2)}, u32[]{:S(2)}) %collective-permute-start.10) | collective-permute-done | bytes 262176 | tf_op jit(solution)/shard_map/ppermute | solution.py:91
  72.3 6.7 %collective-permute-done.4 = bf16[128,512]{1,0:T(8,128)(2,1)S(1)} collective-permute-done((bf16[128,512]{1,0:T(8,128)(2,1)S(1)}, bf16[128,512]{1,0:T(8,128)(2,1)S(1)}, u32[]{:S(2)}, u32[]{:S(2)}) %collective-permute-start.4) | collective-permute-done | bytes 131104 | tf_op jit(solution)/shard_map/ppermute | solution.py:64
  84.4 5.1 %collective-permute-done.12.refs_5_ = bf16[864,128]{1,0:T(8,128)(2,1)S(1)} collective-permute-done((bf16[864,128]{1,0:T(8,128)(2,1)S(1)}, bf16[864,128]{1,0:T(8,128)(2,1)S(1)}, u32[]{:S(2)}, u32[]{:S(2)}) %collective-permute-start.12) | collective-permute-done | bytes 221216 | tf_op jit(solution)/shard_map/ppermute | solution.py:64
  89.8 8.4 %collective-permute-done.13.refs_6_ = bf16[864,128]{1,0:T(8,128)(2,1)S(1)} collective-permute-done((bf16[864,128]{1,0:T(8,128)(2,1)S(1)}, bf16[864,128]{1,0:T(8,128)(2,1)S(1)}, u32[]{:S(2)}, u32[]{:S(2)}) %collective-permute-start.13) | collective-permute-done | bytes 221216 | tf_op jit(solution)/shard_map/ppermute | solution.py:64
  100.3 6.2 %collective-permute-done.17.refs_10_ = bf16[864,128]{1,0:T(8,128)(2,1)S(1)} collective-permute-done((bf16[864,128]{1,0:T(8,128)(2,1)S(1)}, bf16[864,128]{1,0:T(8,128)(2,1)S(1)}, u32[]{:S(2)}, u32[]{:S(2)}) %collective-permute-start.17) | collective-permute-done | bytes 221216 | tf_op jit(solution)/shard_map/ppermute | solution.py:91
  108.9 7.4 %ffn.1 = (bf16[4,2,128,256]{3,2,1,0:T(8,128)(2,1)S(1)}, bf16[4,2,128,256]{3,2,1,0:T(8,128)(2,1)S(1)}, bf16[4,2,128,256]{3,2,1,0:T(8,128)(2,1)S(1)}, bf16[4,2,128...) custom-call(s32[3]{0:T(128)S(1)} %pad_add_fusion.at, ...), custom_call_target="tpu_custom_call" | custom-call | tf_op jit(solution)/shard_map/ffn/pallas_call | solution.py:243
  119.2 9.0 %all-to-all-start.2 = ((bf16[8,128,256]{2,1,0:T(8,128)(2,1)}), bf16[8,128,256]{2,1,0:T(8,128)(2,1)}, u32[]{:S(2)}, u32[]{:S(2)}) async-start(bf16[8,128,256]{2,1,0:T(8,128)(2,1)} %bitcast.253), calls=%async_computation.2 | async-start | bytes 1048576 | tf_op jit(solution)/shard_map/all_to_all | solution.py:59
  129.4 9.3 %collective-permute-done.21 = bf16[4,864,128]{2,1,0:T(8,128)(2,1)} collective-permute-done((bf16[4,864,128]{2,1,0:T(8,128)(2,1)}, bf16[4,864,128]{2,1,0:T(8,128)(2,1)}, u32[]{:S(2)}, u32[]{:S(2)}) %collective-permute-start.21) | collective-permute-done | bytes 884768 | tf_op jit(solution)/shard_map/ppermute | solution.py:91
  153.0 3.4 %collective-permute-start.27 = (bf16[864,128]{1,0:T(8,128)(2,1)S(1)}, bf16[864,128]{1,0:T(8,128)(2,1)S(1)}, u32[]{:S(2)}, u32[]{:S(2)}) collective-permute-start(bf16[864,128]{1,0:T(8,128)(2,1)S(1)} %copy-done.41), channel_id=1, source_target_pairs={{0,16},{8,24},{16,0},{24,8},{1,17},{9,25},{17,1},{25,9},{2,18},{10... | collective-permute-start | bytes 663560 | tf_op jit(solution)/shard_map/ppermute | solution.py:64
  160.7 3.4 %collective-permute-start.24 = (bf16[128,256]{1,0:T(8,128)(2,1)S(1)}, bf16[128,256]{1,0:T(8,128)(2,1)S(1)}, u32[]{:S(2)}, u32[]{:S(2)}) collective-permute-start(bf16[128,256]{1,0:T(8,128)(2,1)S(1)} %get-tuple-element.152), channel_id=1, source_target_pairs={{0,16},{8,24},{16,0},{24,8},{1,17},{9,25},{17,1},{25,9},{2,18},{10... | collective-permute-start | bytes 196616 | tf_op jit(solution)/shard_map/ppermute | solution.py:64
  166.4 5.3 %collective-permute-done.27 = bf16[864,128]{1,0:T(8,128)(2,1)S(1)} collective-permute-done((bf16[864,128]{1,0:T(8,128)(2,1)S(1)}, bf16[864,128]{1,0:T(8,128)(2,1)S(1)}, u32[]{:S(2)}, u32[]{:S(2)}) %collective-permute-start.27) | collective-permute-done | bytes 221216 | tf_op jit(solution)/shard_map/ppermute | solution.py:64
  173.2 7.0 %collective-permute-done.24 = bf16[128,256]{1,0:T(8,128)(2,1)S(1)} collective-permute-done((bf16[128,256]{1,0:T(8,128)(2,1)S(1)}, bf16[128,256]{1,0:T(8,128)(2,1)S(1)}, u32[]{:S(2)}, u32[]{:S(2)}) %collective-permute-start.24) | collective-permute-done | bytes 65568 | tf_op jit(solution)/shard_map/ppermute | solution.py:64
  184.6 4.3 %multiply_subtract_fusion = (f32[2,128,1152]{2,1,0:T(8,128)}, f32[2,128,1152]{2,1,0:T(8,128)}, f32[2,128,1152]{2,1,0:T(8,128)}, f32[2,128,1152]{2,1,0:T(8,128)}) fusion(f32[2,128,1152]{2,1,0:T(8,128)S(1)} %copy-done.2, f32[2,128,1152]{2,1,0:T(8,128)} %param.46, f32[2,128,1152]{2,1,0:T(8,128)} %param.39, bf16[2,1152,128]{1,2,0:T(8,128)(2,1)} %copy.150), kind=kLoop, calls=%fused_computation.10 | loop fusion | flops 4718592 | bytes 8847360 | tf_op jit(solution)/shard_map/sub | solution.py:55
  199.7 3.0 %collective-permute-start.38 = (bf16[2,512,128]{2,1,0:T(8,128)(2,1)}, bf16[2,512,128]{2,1,0:T(8,128)(2,1)}, u32[]{:S(2)}, u32[]{:S(2)}) collective-permute-start(bf16[2,512,128]{2,1,0:T(8,128)(2,1)} %get-tuple-element.119), channel_id=1, source_target_pairs={{0,24},{8,0},{16,8},{24,16},{1,25},{9,1},{17,9},{25,17},{2,26},{10... | collective-permute-start | bytes 786440 | tf_op jit(solution)/shard_map/ppermute | solution.py:64
  206.8 4.1 %all-to-all-start.3 = ((bf16[8,128,256]{2,1,0:T(8,128)(2,1)}), bf16[8,128,256]{2,1,0:T(8,128)(2,1)}, u32[]{:S(2)}, u32[]{:S(2)}) async-start(bf16[8,128,256]{2,1,0:T(8,128)(2,1)} %bitcast.65), calls=%async_computation.3 | async-start | bytes 1048576 | tf_op jit(solution)/shard_map/all_to_all | solution.py:59
  211.1 15.9 %collective-permute-done.37 = bf16[2,512,128]{2,1,0:T(8,128)(2,1)} collective-permute-done((bf16[2,512,128]{2,1,0:T(8,128)(2,1)}, bf16[2,512,128]{2,1,0:T(8,128)(2,1)}, u32[]{:S(2)}, u32[]{:S(2)}) %collective-permute-start.37) | collective-permute-done | bytes 262176 | tf_op jit(solution)/shard_map/ppermute | solution.py:64
  229.7 3.6 %collective-permute-done.39 = bf16[512,128]{1,0:T(8,128)(2,1)S(1)} collective-permute-done((bf16[512,128]{1,0:T(8,128)(2,1)S(1)}, bf16[512,128]{1,0:T(8,128)(2,1)S(1)}, u32[]{:S(2)}, u32[]{:S(2)}) %collective-permute-start.39) | collective-permute-done | bytes 131104 | tf_op jit(solution)/shard_map/ppermute | solution.py:91
  241.8 3.3 %all-to-all-start.4 = ((f32[8,1,640]{2,1,0:T(1,128)}), f32[8,1,640]{2,1,0:T(1,128)S(1)}, u32[]{:S(2)}, u32[]{:S(2)}) async-start(f32[8,1,640]{2,1,0:T(1,128)} %all_to_all.22), calls=%async_computation.4 | async-start | bytes 40960 | tf_op jit(solution)/shard_map/all_to_all | solution.py:59
  246.6 5.1 %all-to-all-done.4 = f32[8,1,640]{2,1,0:T(1,128)S(1)} async-done(((f32[8,1,640]{2,1,0:T(1,128)}), f32[8,1,640]{2,1,0:T(1,128)S(1)}, u32[]{:S(2)}, u32[]{:S(2)}) %all-to-all-start.4) | async-done | bytes 20512 | tf_op jit(solution)/shard_map/all_to_all | solution.py:59
  (336 shorter events, 107.0 us)
Async XLA Ops:
  5.7 33.6 %all-to-all-start = ((bf16[8,514,128]{2,1,0:T(8,128)(2,1)}), bf16[8,514,128]{2,1,0:T(8,128)(2,1)S(1)}, u32[]{:S(2)}, u32[]{:S(2)}) async-start(bf16[8,514,128]{2,1,0:T(8,128)(2,1)} %bitcast.5), calls=%async_computation | async-start | bytes 2129920 | tf_op jit(solution)/shard_map/all_to_all | solution.py:59
  13.4 17.7 %collective-permute-start = (bf16[128,1024]{1,0:T(8,128)(2,1)S(1)}, bf16[128,1024]{1,0:T(8,128)(2,1)}, u32[]{:S(2)}, u32[]{:S(2)}) collective-permute-start(bf16[128,1024]{1,0:T(8,128)(2,1)S(1)} %fusion.20), channel_id=1, source_target_pairs={{0,4},{4,0},{1,5},{5,1},{2,6},{6,2},{3,7},{7,3},{8,12},{12,8},{9,1... | collective-permute-start | bytes 786440 | tf_op jit(solution)/shard_map/ppermute | solution.py:91
  45.8 13.0 %all-to-all-start.1 = ((bf16[8,128,256]{2,1,0:T(8,128)(2,1)}), bf16[8,128,256]{2,1,0:T(8,128)(2,1)S(1)}, u32[]{:S(2)}, u32[]{:S(2)}) async-start(bf16[8,128,256]{2,1,0:T(8,128)(2,1)} %bitcast.35), calls=%async_computation.1 | async-start | bytes 1048576 | tf_op jit(solution)/shard_map/all_to_all | solution.py:59
  49.4 32.1 %collective-permute-start.15 = (bf16[864,128]{1,0:T(8,128)(2,1)S(1)}, bf16[864,128]{1,0:T(8,128)(2,1)S(1)}, u32[]{:S(2)}, u32[]{:S(2)}) collective-permute-start(bf16[864,128]{1,0:T(8,128)(2,1)S(1)} %get-tuple-element.58.refs_4_), channel_id=1, source_target_pairs={{0,4},{4,0},{1,5},{5,1},{2,6},{6,2},{3,7},{7,3},{8,12},{12,8},{9,1... | collective-permute-start | bytes 663560 | tf_op jit(solution)/shard_map/ppermute | solution.py:91
  51.4 11.9 %collective-permute-start.8 = (bf16[128,256]{1,0:T(8,128)(2,1)S(1)}, bf16[128,256]{1,0:T(8,128)(2,1)S(1)}, u32[]{:S(2)}, u32[]{:S(2)}) collective-permute-start(bf16[128,256]{1,0:T(8,128)(2,1)S(1)} %dynamic-slice_convert_fusion.1), channel_id=1, source_target_pairs={{0,16},{8,24},{16,0},{24,8},{1,17},{9,25},{17,1},{25,9},{2,18},{10... | collective-permute-start | bytes 196616 | tf_op jit(solution)/shard_map/ppermute | solution.py:64
  67.2 11.8 %collective-permute-start.4 = (bf16[128,512]{1,0:T(8,128)(2,1)S(1)}, bf16[128,512]{1,0:T(8,128)(2,1)S(1)}, u32[]{:S(2)}, u32[]{:S(2)}) collective-permute-start(bf16[128,512]{1,0:T(8,128)(2,1)S(1)} %fusion.23), channel_id=1, source_target_pairs={{0,16},{8,24},{16,0},{24,8},{1,17},{9,25},{17,1},{25,9},{2,18},{10... | collective-permute-start | bytes 393224 | tf_op jit(solution)/shard_map/ppermute | solution.py:64
  67.2 11.8 %collective-permute-start.3 = (bf16[128,512]{1,0:T(8,128)(2,1)S(1)}, bf16[128,512]{1,0:T(8,128)(2,1)S(1)}, u32[]{:S(2)}, u32[]{:S(2)}) collective-permute-start(bf16[128,512]{1,0:T(8,128)(2,1)S(1)} %fusion.23), channel_id=1, source_target_pairs={{0,8},{8,16},{16,24},{24,0},{1,9},{9,17},{17,25},{25,1},{2,10},{10... | collective-permute-start | bytes 393224 | tf_op jit(solution)/shard_map/ppermute | solution.py:64
  72.2 36.6 %collective-permute-start.11 = (bf16[512,512]{1,0:T(8,128)(2,1)S(1)}, bf16[512,512]{1,0:T(8,128)(2,1)S(1)}, u32[]{:S(2)}, u32[]{:S(2)}) collective-permute-start(bf16[512,512]{1,0:T(8,128)(2,1)S(1)} %pad_maximum_fusion.4.refs_2_), channel_id=1, source_target_pairs={{0,1},{1,0},{2,3},{3,2},{4,5},{5,4},{6,7},{7,6},{8,9},{9,8},{10,11... | collective-permute-start | bytes 1572872 | tf_op jit(solution)/shard_map/ppermute | solution.py:91
  79.0 29.8 %collective-permute-start.6 = (bf16[512,512]{1,0:T(8,128)(2,1)S(1)}, bf16[512,512]{1,0:T(8,128)(2,1)S(1)}, u32[]{:S(2)}, u32[]{:S(2)}) collective-permute-start(bf16[512,512]{1,0:T(8,128)(2,1)S(1)} %pad_maximum_fusion.3.refs_0_), channel_id=1, source_target_pairs={{0,1},{1,0},{2,3},{3,2},{4,5},{5,4},{6,7},{7,6},{8,9},{9,8},{10,11... | collective-permute-start | bytes 1572872 | tf_op jit(solution)/shard_map/ppermute | solution.py:91
  79.5 18.7 %collective-permute-start.13 = (bf16[864,128]{1,0:T(8,128)(2,1)S(1)}, bf16[864,128]{1,0:T(8,128)(2,1)S(1)}, u32[]{:S(2)}, u32[]{:S(2)}) collective-permute-start(bf16[864,128]{1,0:T(8,128)(2,1)S(1)} %copy-done.44), channel_id=1, source_target_pairs={{0,16},{8,24},{16,0},{24,8},{1,17},{9,25},{17,1},{25,9},{2,18},{10... | collective-permute-start | bytes 663560 | tf_op jit(solution)/shard_map/ppermute | solution.py:64
  81.5 17.1 %collective-permute-start.14 = (bf16[864,128]{1,0:T(8,128)(2,1)S(1)}, bf16[864,128]{1,0:T(8,128)(2,1)S(1)}, u32[]{:S(2)}, u32[]{:S(2)}) collective-permute-start(bf16[864,128]{1,0:T(8,128)(2,1)S(1)} %copy-done.43), channel_id=1, source_target_pairs={{0,24},{8,0},{16,8},{24,16},{1,25},{9,1},{17,9},{25,17},{2,26},{10... | collective-permute-start | bytes 663560 | tf_op jit(solution)/shard_map/ppermute | solution.py:64
  116.3 22.4 %collective-permute-start.21 = (bf16[4,864,128]{2,1,0:T(8,128)(2,1)}, bf16[4,864,128]{2,1,0:T(8,128)(2,1)}, u32[]{:S(2)}, u32[]{:S(2)}) collective-permute-start(bf16[4,864,128]{2,1,0:T(8,128)(2,1)} %get-tuple-element.67), channel_id=1, source_target_pairs={{0,4},{4,0},{1,5},{5,1},{2,6},{6,2},{3,7},{7,3},{8,12},{12,8},{9,1... | collective-permute-start | bytes 2654216 | tf_op jit(solution)/shard_map/ppermute | solution.py:91
  119.2 23.9 %all-to-all-start.2 = ((bf16[8,128,256]{2,1,0:T(8,128)(2,1)}), bf16[8,128,256]{2,1,0:T(8,128)(2,1)}, u32[]{:S(2)}, u32[]{:S(2)}) async-start(bf16[8,128,256]{2,1,0:T(8,128)(2,1)} %bitcast.253), calls=%async_computation.2 | async-start | bytes 1048576 | tf_op jit(solution)/shard_map/all_to_all | solution.py:59
  151.1 13.0 %collective-permute-start.26 = (bf16[864,128]{1,0:T(8,128)(2,1)S(1)}, bf16[864,128]{1,0:T(8,128)(2,1)S(1)}, u32[]{:S(2)}, u32[]{:S(2)}) collective-permute-start(bf16[864,128]{1,0:T(8,128)(2,1)S(1)} %copy-done.42), channel_id=1, source_target_pairs={{0,8},{8,16},{16,24},{24,0},{1,9},{9,17},{17,25},{25,1},{2,10},{10... | collective-permute-start | bytes 663560 | tf_op jit(solution)/shard_map/ppermute | solution.py:64
  153.0 18.7 %collective-permute-start.27 = (bf16[864,128]{1,0:T(8,128)(2,1)S(1)}, bf16[864,128]{1,0:T(8,128)(2,1)S(1)}, u32[]{:S(2)}, u32[]{:S(2)}) collective-permute-start(bf16[864,128]{1,0:T(8,128)(2,1)S(1)} %copy-done.41), channel_id=1, source_target_pairs={{0,16},{8,24},{16,0},{24,8},{1,17},{9,25},{17,1},{25,9},{2,18},{10... | collective-permute-start | bytes 663560 | tf_op jit(solution)/shard_map/ppermute | solution.py:64
  156.4 15.6 %collective-permute-start.28 = (bf16[864,128]{1,0:T(8,128)(2,1)S(1)}, bf16[864,128]{1,0:T(8,128)(2,1)S(1)}, u32[]{:S(2)}, u32[]{:S(2)}) collective-permute-start(bf16[864,128]{1,0:T(8,128)(2,1)S(1)} %copy-done.40), channel_id=1, source_target_pairs={{0,24},{8,0},{16,8},{24,16},{1,25},{9,1},{17,9},{25,17},{2,26},{10... | collective-permute-start | bytes 663560 | tf_op jit(solution)/shard_map/ppermute | solution.py:64
  158.4 14.7 %collective-permute-start.23 = (bf16[128,256]{1,0:T(8,128)(2,1)S(1)}, bf16[128,256]{1,0:T(8,128)(2,1)S(1)}, u32[]{:S(2)}, u32[]{:S(2)}) collective-permute-start(bf16[128,256]{1,0:T(8,128)(2,1)S(1)} %get-tuple-element.153), channel_id=1, source_target_pairs={{0,8},{8,16},{16,24},{24,0},{1,9},{9,17},{17,25},{25,1},{2,10},{10... | collective-permute-start | bytes 196616 | tf_op jit(solution)/shard_map/ppermute | solution.py:64
  160.7 19.5 %collective-permute-start.24 = (bf16[128,256]{1,0:T(8,128)(2,1)S(1)}, bf16[128,256]{1,0:T(8,128)(2,1)S(1)}, u32[]{:S(2)}, u32[]{:S(2)}) collective-permute-start(bf16[128,256]{1,0:T(8,128)(2,1)S(1)} %get-tuple-element.152), channel_id=1, source_target_pairs={{0,16},{8,24},{16,0},{24,8},{1,17},{9,25},{17,1},{25,9},{2,18},{10... | collective-permute-start | bytes 196616 | tf_op jit(solution)/shard_map/ppermute | solution.py:64
  164.1 16.1 %collective-permute-start.25 = (bf16[128,256]{1,0:T(8,128)(2,1)S(1)}, bf16[128,256]{1,0:T(8,128)(2,1)S(1)}, u32[]{:S(2)}, u32[]{:S(2)}) collective-permute-start(bf16[128,256]{1,0:T(8,128)(2,1)S(1)} %get-tuple-element.151), channel_id=1, source_target_pairs={{0,24},{8,0},{16,8},{24,16},{1,25},{9,1},{17,9},{25,17},{2,26},{10... | collective-permute-start | bytes 196616 | tf_op jit(solution)/shard_map/ppermute | solution.py:64
  171.7 19.4 %collective-permute-start.31 = (bf16[128,1024]{1,0:T(8,128)(2,1)}, bf16[128,1024]{1,0:T(8,128)(2,1)}, u32[]{:S(2)}, u32[]{:S(2)}) collective-permute-start(bf16[128,1024]{1,0:T(8,128)(2,1)} %fusion.10), channel_id=1, source_target_pairs={{0,4},{4,0},{1,5},{5,1},{2,6},{6,2},{3,7},{7,3},{8,12},{12,8},{9,1... | collective-permute-start | bytes 786440 | tf_op jit(solution)/shard_map/ppermute | solution.py:91
  191.2 37.5 %collective-permute-start.33 = (bf16[128,512]{1,0:T(8,128)(2,1)}, bf16[128,512]{1,0:T(8,128)(2,1)}, u32[]{:S(2)}, u32[]{:S(2)}) collective-permute-start(bf16[128,512]{1,0:T(8,128)(2,1)} %pad_maximum_fusion.15), channel_id=1, source_target_pairs={{0,1},{1,0},{2,3},{3,2},{4,5},{5,4},{6,7},{7,6},{8,9},{9,8},{10,11... | collective-permute-start | bytes 393224 | tf_op jit(solution)/shard_map/ppermute | solution.py:91
  202.7 24.2 %collective-permute-start.37 = (bf16[2,512,128]{2,1,0:T(8,128)(2,1)}, bf16[2,512,128]{2,1,0:T(8,128)(2,1)}, u32[]{:S(2)}, u32[]{:S(2)}) collective-permute-start(bf16[2,512,128]{2,1,0:T(8,128)(2,1)} %get-tuple-element.120), channel_id=1, source_target_pairs={{0,16},{8,24},{16,0},{24,8},{1,17},{9,25},{17,1},{25,9},{2,18},{10... | collective-permute-start | bytes 786440 | tf_op jit(solution)/shard_map/ppermute | solution.py:64
  203.1 23.9 %collective-permute-start.36 = (bf16[2,512,128]{2,1,0:T(8,128)(2,1)S(1)}, bf16[2,512,128]{2,1,0:T(8,128)(2,1)}, u32[]{:S(2)}, u32[]{:S(2)}) collective-permute-start(bf16[2,512,128]{2,1,0:T(8,128)(2,1)S(1)} %get-tuple-element.118), channel_id=1, source_target_pairs={{0,8},{8,16},{16,24},{24,0},{1,9},{9,17},{17,25},{25,1},{2,10},{10... | collective-permute-start | bytes 786440 | tf_op jit(solution)/shard_map/ppermute | solution.py:64
  206.8 26.6 %all-to-all-start.3 = ((bf16[8,128,256]{2,1,0:T(8,128)(2,1)}), bf16[8,128,256]{2,1,0:T(8,128)(2,1)}, u32[]{:S(2)}, u32[]{:S(2)}) async-start(bf16[8,128,256]{2,1,0:T(8,128)(2,1)} %bitcast.65), calls=%async_computation.3 | async-start | bytes 1048576 | tf_op jit(solution)/shard_map/all_to_all | solution.py:59
  (90 other events, 502.6 us)

commit v2 on v1

--- a/solution.py
+++ b/solution.py
@@ -104,7 +104,8 @@
         mine = lax.axis_index(axis)
         kept = lax.dynamic_index_in_dim(blocks, mine, 0, keepdims=False)
         given = lax.dynamic_index_in_dim(blocks, 1 - mine, 0, keepdims=False)
-        return kept.astype(f32) + swap(given, axis).astype(f32)
+        given = swap(given, axis)
+        return kept.astype(f32) + given.astype(f32)
     return jnp.sum(exchange(blocks, axis).astype(f32), axis=0)
 
 
@@ -421,7 +422,6 @@
         grad_ffn = by_distance(sum_scatter(grad_ffn, "ctx").astype(bf16))
 
     grad_part = exchange(grad_part.reshape(n_dp * n_hi, count, quarter), ("dp", "hi"))
-    grad_part, ffn_part, grad_ffn = lax.optimization_barrier((grad_part, ffn_part, grad_ffn))
     grad_ffn = send_each(grad_ffn)
     grad_part = jnp.sum(grad_part.astype(f32), axis=0).astype(bf16)
     grad_normed_two = gather_features(grad_part).astype(f32)
@@ -456,13 +456,21 @@
             (grad_mixed * gate_b).astype(bf16),
         ]
     )
-    ffn_part, grad_ffn, _ = lax.optimization_barrier((ffn_part, grad_ffn, grad_gates))
-    ffn_part = functools.reduce(jnp.add, [part.astype(f32) for part in ffn_part]).astype(bf16)
-    result = hidden_rows + gather_features(ffn_part).astype(f32)
     grad_ffn = by_member(grad_ffn).reshape(n_dp, 3, f_own, d_own).transpose(1, 0, 2, 3)
     grad_ffn = grad_ffn.reshape(3, f_tp, d_own)
     owned_gate_up = row_major(grad_ffn[:2].transpose(0, 2, 1)).astype(f32)
     owned_down = grad_ffn[2].astype(f32)
+    steps = jnp.float32(STEP)
+    bias_one = 1.0 - jnp.power(jnp.float32(BETA_ONE), steps)
+    bias_two = 1.0 - jnp.power(jnp.float32(BETA_TWO), steps)
+    new_gate_up, new_first_gate_up, new_second_gate_up = adamw(
+        gate_up_weight, owned_gate_up, first_gate_up, second_gate_up, bias_one, bias_two
+    )
+    new_down, new_first_down, new_second_down = adamw(
+        down_weight, owned_down, first_down, second_down, bias_one, bias_two
+    )
+    ffn_part = functools.reduce(jnp.add, [part.astype(f32) for part in ffn_part]).astype(bf16)
+    result = hidden_rows + gather_features(ffn_part).astype(f32)
 
     grad_in = jnp.einsum("td,ktc->kdc", normed_seq, grad_gates, preferred_element_type=f32)
     grad_mixer = jnp.concatenate([grad_in.astype(bf16), grad_out.astype(bf16)[None]])
@@ -504,29 +512,20 @@
     grad_conv = small[:, 2 * d_own :].reshape(n_ctx, 3, c_own)
     grad_conv = grad_conv.transpose(1, 0, 2).reshape(3, c_tp)
 
-    steps = jnp.float32(STEP)
-    bias_one = 1.0 - jnp.power(jnp.float32(BETA_ONE), steps)
-    bias_two = 1.0 - jnp.power(jnp.float32(BETA_TWO), steps)
     new_norm1, new_first_norm1, new_second_norm1 = adamw(
         norm1_gain, owned_norm1, first_norm1, second_norm1, bias_one, bias_two
     )
     new_in, new_first_in, new_second_in = adamw(
         in_weight, owned_in, first_in, second_in, bias_one, bias_two
     )
+    new_out, new_first_out, new_second_out = adamw(
+        out_weight, owned_out, first_out, second_out, bias_one, bias_two
+    )
     new_conv, new_first_conv, new_second_conv = adamw(
         conv_weight, grad_conv, first_conv, second_conv, bias_one, bias_two
     )
-    new_out, new_first_out, new_second_out = adamw(
-        out_weight, owned_out, first_out, second_out, bias_one, bias_two
-    )
     new_norm2, new_first_norm2, new_second_norm2 = adamw(
         norm2_gain, owned_norm2, first_norm2, second_norm2, bias_one, bias_two
-    )
-    new_gate_up, new_first_gate_up, new_second_gate_up = adamw(
-        gate_up_weight, owned_gate_up, first_gate_up, second_gate_up, bias_one, bias_two
-    )
-    new_down, new_first_down, new_second_down = adamw(
-        down_weight, owned_down, first_down, second_down, bias_one, bias_two
     )
     return (
         result.reshape(tokens.shape),

time: 255 us -> 258 us (1.012)
  waiting for transfers between devices: 110 us -> 130 us
  other arithmetic: 35.8 us -> 27.3 us
  local copies, waits for them, and re-layouts: 21.9 us -> 17.9 us
  starting transfers between devices: 72.7 us -> 68.9 us
    ppermute x18, waiting for transfers between devices: 49.5 us -> 60.1 us  [shift(): return lax.ppermute(block, 'dp', [(i, (i + k) % n) for i in range(n)])]
    all_to_all x5, waiting for transfers between devices: 16.9 us -> 25 us  [exchange(): return lax.all_to_all(blocks, axes, 0, 0, tiled=True)]
    all_to_all x5, starting transfers between devices: 27.5 us -> 23.3 us  [exchange(): return lax.all_to_all(blocks, axes, 0, 0, tiled=True)]
  transfers between devices with their start and end apart: 45 -> 45, of which waited for: 22 -> 23; matrix products, arithmetic and copies ran while one was open for 17% -> 10% of each run, Pallas kernels for 0% -> 0%
where the time goes in v2:
time: 258 us; the launch traced here: 257 us
  waiting for transfers between devices  130 us (50%)
  starting transfers between devices  68.9 us (27%)
  other arithmetic  27.3 us (11%)
  local copies, waits for them, and re-layouts  17.9 us (7%)
  Pallas kernels  7.44 us (3%)
    ppermute x18, waiting for transfers between devices, shift(): return lax.ppermute(block, 'dp', [(i, (i + k) % n) for i in range(n)])  60.1 us
    ppermute x22, waiting for transfers between devices, swap(): return lax.ppermute(block, axis, [(0, 1), (1, 0)])  45.4 us
    ppermute x18, starting transfers between devices, shift(): return lax.ppermute(block, 'dp', [(i, (i + k) % n) for i in range(n)])  27.1 us
    all_to_all x5, waiting for transfers between devices, exchange(): return lax.all_to_all(blocks, axes, 0, 0, tiled=True)  25 us
    all_to_all x5, starting transfers between devices, exchange(): return lax.all_to_all(blocks, axes, 0, 0, tiled=True)  23.3 us
    ppermute x22, starting transfers between devices, swap(): return lax.ppermute(block, axis, [(0, 1), (1, 0)])  18.6 us
    sub x7, other arithmetic, adamw(): return (param - LEARN_RATE * update, new_first, new_second)  8.93 us
    pallas_call x1, Pallas kernels, ffn_kernel(): pl.pallas_call(functools.partial(ffn_body, n_dp), out_shape=(parts, parts...  7.44 us
  transfers between devices with their start and end apart: 45, of which 23 were waited for; matrix products, arithmetic and copies ran while one was open for 10% of the time, Pallas kernels for 0%

profile of v2, /device:TPU:0, one launch (start us, length us, event | category | flops | bytes accessed | tf_op | source)
XLA Modules:
  0.0 256.6 jit_solution(7845422036153676812)
XLA Ops:
  5.7 7.4 %all-to-all-start = ((bf16[8,514,128]{2,1,0:T(8,128)(2,1)}), bf16[8,514,128]{2,1,0:T(8,128)(2,1)}, u32[]{:S(2)}, u32[]{:S(2)}) async-start(bf16[8,514,128]{2,1,0:T(8,128)(2,1)} %bitcast.5), calls=%async_computation | async-start | bytes 2129920 | tf_op jit(solution)/shard_map/all_to_all | solution.py:59
  19.3 11.8 %collective-permute-done = bf16[128,1024]{1,0:T(8,128)(2,1)S(1)} collective-permute-done((bf16[128,1024]{1,0:T(8,128)(2,1)S(1)}, bf16[128,1024]{1,0:T(8,128)(2,1)S(1)}, u32[]{:S(2)}, u32[]{:S(2)}) %collective-permute-start) | collective-permute-done | bytes 262176 | tf_op jit(solution)/shard_map/ppermute | solution.py:91
  31.9 7.5 %all-to-all-done = bf16[8,514,128]{2,1,0:T(8,128)(2,1)} async-done(((bf16[8,514,128]{2,1,0:T(8,128)(2,1)}), bf16[8,514,128]{2,1,0:T(8,128)(2,1)}, u32[]{:S(2)}, u32[]{:S(2)}) %all-to-all-start) | async-done | bytes 1052704 | tf_op jit(solution)/shard_map/all_to_all | solution.py:59
  46.5 3.6 %all-to-all-start.1 = ((bf16[8,128,256]{2,1,0:T(8,128)(2,1)}), bf16[8,128,256]{2,1,0:T(8,128)(2,1)S(1)}, u32[]{:S(2)}, u32[]{:S(2)}) async-start(bf16[8,128,256]{2,1,0:T(8,128)(2,1)} %bitcast.35), calls=%async_computation.1 | async-start | bytes 1048576 | tf_op jit(solution)/shard_map/all_to_all | solution.py:59
  68.5 4.3 %collective-permute-done.10 = bf16[512,256]{1,0:T(8,128)(2,1)S(1)} collective-permute-done((bf16[512,256]{1,0:T(8,128)(2,1)S(1)}, bf16[512,256]{1,0:T(8,128)(2,1)S(1)}, u32[]{:S(2)}, u32[]{:S(2)}) %collective-permute-start.10) | collective-permute-done | bytes 262176 | tf_op jit(solution)/shard_map/ppermute | solution.py:91
  73.1 6.7 %collective-permute-done.4 = bf16[128,512]{1,0:T(8,128)(2,1)S(1)} collective-permute-done((bf16[128,512]{1,0:T(8,128)(2,1)S(1)}, bf16[128,512]{1,0:T(8,128)(2,1)S(1)}, u32[]{:S(2)}, u32[]{:S(2)}) %collective-permute-start.4) | collective-permute-done | bytes 131104 | tf_op jit(solution)/shard_map/ppermute | solution.py:64
  85.1 5.1 %collective-permute-done.12.refs_5_ = bf16[864,128]{1,0:T(8,128)(2,1)S(1)} collective-permute-done((bf16[864,128]{1,0:T(8,128)(2,1)S(1)}, bf16[864,128]{1,0:T(8,128)(2,1)S(1)}, u32[]{:S(2)}, u32[]{:S(2)}) %collective-permute-start.12) | collective-permute-done | bytes 221216 | tf_op jit(solution)/shard_map/ppermute | solution.py:64
  90.6 8.4 %collective-permute-done.13.refs_6_ = bf16[864,128]{1,0:T(8,128)(2,1)S(1)} collective-permute-done((bf16[864,128]{1,0:T(8,128)(2,1)S(1)}, bf16[864,128]{1,0:T(8,128)(2,1)S(1)}, u32[]{:S(2)}, u32[]{:S(2)}) %collective-permute-start.13) | collective-permute-done | bytes 221216 | tf_op jit(solution)/shard_map/ppermute | solution.py:64
  101.1 6.2 %collective-permute-done.17.refs_10_ = bf16[864,128]{1,0:T(8,128)(2,1)S(1)} collective-permute-done((bf16[864,128]{1,0:T(8,128)(2,1)S(1)}, bf16[864,128]{1,0:T(8,128)(2,1)S(1)}, u32[]{:S(2)}, u32[]{:S(2)}) %collective-permute-start.17) | collective-permute-done | bytes 221216 | tf_op jit(solution)/shard_map/ppermute | solution.py:91
  109.7 7.4 %ffn.1 = (bf16[4,2,128,256]{3,2,1,0:T(8,128)(2,1)S(1)}, bf16[4,2,128,256]{3,2,1,0:T(8,128)(2,1)S(1)}, bf16[4,2,128,256]{3,2,1,0:T(8,128)(2,1)S(1)}, bf16[4,2,128...) custom-call(s32[3]{0:T(128)S(1)} %pad_add_fusion.at, ...), custom_call_target="tpu_custom_call" | custom-call | tf_op jit(solution)/shard_map/ffn/pallas_call | solution.py:244
  123.5 6.3 %collective-permute-done.20 = bf16[4,128,256]{2,1,0:T(8,128)(2,1)S(1)} collective-permute-done((bf16[4,128,256]{2,1,0:T(8,128)(2,1)S(1)}, bf16[4,128,256]{2,1,0:T(8,128)(2,1)S(1)}, u32[]{:S(2)}, u32[]{:S(2)}) %collective-permute-start.20) | collective-permute-done | bytes 262176 | tf_op jit(solution)/shard_map/ppermute | solution.py:91
  129.9 7.3 %collective-permute-start.23 = (bf16[128,256]{1,0:T(8,128)(2,1)S(1)}, bf16[128,256]{1,0:T(8,128)(2,1)S(1)}, u32[]{:S(2)}, u32[]{:S(2)}) collective-permute-start(bf16[128,256]{1,0:T(8,128)(2,1)S(1)} %get-tuple-element.124), channel_id=1, source_target_pairs={{0,24},{8,0},{16,8},{24,16},{1,25},{9,1},{17,9},{25,17},{2,26},{10... | collective-permute-start | bytes 196616 | tf_op jit(solution)/shard_map/ppermute | solution.py:64
  139.3 4.7 %all-to-all-start.2 = ((bf16[8,128,256]{2,1,0:T(8,128)(2,1)}), bf16[8,128,256]{2,1,0:T(8,128)(2,1)S(1)}, u32[]{:S(2)}, u32[]{:S(2)}) async-start(bf16[8,128,256]{2,1,0:T(8,128)(2,1)} %bitcast.50), calls=%async_computation.2 | async-start | bytes 1048576 | tf_op jit(solution)/shard_map/all_to_all | solution.py:59
  150.1 4.0 %collective-permute-start.39 = (bf16[864,128]{1,0:T(8,128)(2,1)S(1)}, bf16[864,128]{1,0:T(8,128)(2,1)S(1)}, u32[]{:S(2)}, u32[]{:S(2)}) collective-permute-start(bf16[864,128]{1,0:T(8,128)(2,1)S(1)} %get-tuple-element.98), channel_id=1, source_target_pairs={{0,24},{8,0},{16,8},{24,16},{1,25},{9,1},{17,9},{25,17},{2,26},{10... | collective-permute-start | bytes 663560 | tf_op jit(solution)/shard_map/ppermute | solution.py:64
  156.0 4.8 %collective-permute-done.39 = bf16[864,128]{1,0:T(8,128)(2,1)S(1)} collective-permute-done((bf16[864,128]{1,0:T(8,128)(2,1)S(1)}, bf16[864,128]{1,0:T(8,128)(2,1)S(1)}, u32[]{:S(2)}, u32[]{:S(2)}) %collective-permute-start.39) | collective-permute-done | bytes 221216 | tf_op jit(solution)/shard_map/ppermute | solution.py:64
  160.8 15.7 %collective-permute-done.38 = bf16[864,128]{1,0:T(8,128)(2,1)S(1)} collective-permute-done((bf16[864,128]{1,0:T(8,128)(2,1)S(1)}, bf16[864,128]{1,0:T(8,128)(2,1)S(1)}, u32[]{:S(2)}, u32[]{:S(2)}) %collective-permute-start.38) | collective-permute-done | bytes 221216 | tf_op jit(solution)/shard_map/ppermute | solution.py:64
  186.9 3.7 %multiply_subtract_fusion = (f32[2,128,1152]{2,1,0:T(8,128)}, f32[2,128,1152]{2,1,0:T(8,128)}, f32[2,128,1152]{2,1,0:T(8,128)}, f32[2,128,1152]{2,1,0:T(8,128)}) fusion(f32[2,128,1152]{2,1,0:T(8,128)S(1)} %copy-done.2, f32[2,128,1152]{2,1,0:T(8,128)S(1)} %copy-done.24, f32[2,128,1152]{2,1,0:T(8,128)} %param.39, bf16[2,1152,128]{1,2,0:T(8,128)(2,1)S(1)} %copy.162), kind=kLoop, calls=%fused_computation.10 | loop fusion | flops 4718592 | bytes 8847360 | tf_op jit(solution)/shard_map/sub | solution.py:55
  190.6 4.0 %collective-permute-done.29 = bf16[128,1024]{1,0:T(8,128)(2,1)S(1)} collective-permute-done((bf16[128,1024]{1,0:T(8,128)(2,1)S(1)}, bf16[128,1024]{1,0:T(8,128)(2,1)S(1)}, u32[]{:S(2)}, u32[]{:S(2)}) %collective-permute-start.29) | collective-permute-done | bytes 262176 | tf_op jit(solution)/shard_map/ppermute | solution.py:91
  202.1 5.2 %collective-permute-done.34 = bf16[2,512,128]{2,1,0:T(8,128)(2,1)S(1)} collective-permute-done((bf16[2,512,128]{2,1,0:T(8,128)(2,1)S(1)}, bf16[2,512,128]{2,1,0:T(8,128)(2,1)S(1)}, u32[]{:S(2)}, u32[]{:S(2)}) %collective-permute-start.34) | collective-permute-done | bytes 262176 | tf_op jit(solution)/shard_map/ppermute | solution.py:64
  207.3 14.2 %collective-permute-done.33 = bf16[2,512,128]{2,1,0:T(8,128)(2,1)S(1)} collective-permute-done((bf16[2,512,128]{2,1,0:T(8,128)(2,1)S(1)}, bf16[2,512,128]{2,1,0:T(8,128)(2,1)S(1)}, u32[]{:S(2)}, u32[]{:S(2)}) %collective-permute-start.33) | collective-permute-done | bytes 262176 | tf_op jit(solution)/shard_map/ppermute | solution.py:64
  224.4 3.7 %all-to-all-start.3 = ((bf16[8,128,256]{2,1,0:T(8,128)(2,1)}), bf16[8,128,256]{2,1,0:T(8,128)(2,1)S(1)}, u32[]{:S(2)}, u32[]{:S(2)}) async-start(bf16[8,128,256]{2,1,0:T(8,128)(2,1)} %bitcast.61), calls=%async_computation.3 | async-start | bytes 1048576 | tf_op jit(solution)/shard_map/all_to_all | solution.py:59
  228.2 9.0 %all-to-all-done.3 = bf16[8,128,256]{2,1,0:T(8,128)(2,1)S(1)} async-done(((bf16[8,128,256]{2,1,0:T(8,128)(2,1)}), bf16[8,128,256]{2,1,0:T(8,128)(2,1)S(1)}, u32[]{:S(2)}, u32[]{:S(2)}) %all-to-all-start.3) | async-done | bytes 524320 | tf_op jit(solution)/shard_map/all_to_all | solution.py:59
  244.1 3.8 %all-to-all-start.4 = ((f32[8,1,640]{2,1,0:T(1,128)}), f32[8,1,640]{2,1,0:T(1,128)S(1)}, u32[]{:S(2)}, u32[]{:S(2)}) async-start(f32[8,1,640]{2,1,0:T(1,128)} %all_to_all.22), calls=%async_computation.4 | async-start | bytes 40960 | tf_op jit(solution)/shard_map/all_to_all | solution.py:59
  249.4 5.1 %all-to-all-done.4 = f32[8,1,640]{2,1,0:T(1,128)S(1)} async-done(((f32[8,1,640]{2,1,0:T(1,128)}), f32[8,1,640]{2,1,0:T(1,128)S(1)}, u32[]{:S(2)}, u32[]{:S(2)}) %all-to-all-start.4) | async-done | bytes 20512 | tf_op jit(solution)/shard_map/all_to_all | solution.py:59
  (341 shorter events, 94.5 us)
Async XLA Ops:
  5.7 33.7 %all-to-all-start = ((bf16[8,514,128]{2,1,0:T(8,128)(2,1)}), bf16[8,514,128]{2,1,0:T(8,128)(2,1)}, u32[]{:S(2)}, u32[]{:S(2)}) async-start(bf16[8,514,128]{2,1,0:T(8,128)(2,1)} %bitcast.5), calls=%async_computation | async-start | bytes 2129920 | tf_op jit(solution)/shard_map/all_to_all | solution.py:59
  13.4 17.6 %collective-permute-start = (bf16[128,1024]{1,0:T(8,128)(2,1)S(1)}, bf16[128,1024]{1,0:T(8,128)(2,1)S(1)}, u32[]{:S(2)}, u32[]{:S(2)}) collective-permute-start(bf16[128,1024]{1,0:T(8,128)(2,1)S(1)} %fusion.20), channel_id=1, source_target_pairs={{0,4},{4,0},{1,5},{5,1},{2,6},{6,2},{3,7},{7,3},{8,12},{12,8},{9,1... | collective-permute-start | bytes 786440 | tf_op jit(solution)/shard_map/ppermute | solution.py:91
  46.5 13.0 %all-to-all-start.1 = ((bf16[8,128,256]{2,1,0:T(8,128)(2,1)}), bf16[8,128,256]{2,1,0:T(8,128)(2,1)S(1)}, u32[]{:S(2)}, u32[]{:S(2)}) async-start(bf16[8,128,256]{2,1,0:T(8,128)(2,1)} %bitcast.35), calls=%async_computation.1 | async-start | bytes 1048576 | tf_op jit(solution)/shard_map/all_to_all | solution.py:59
  50.2 32.1 %collective-permute-start.15 = (bf16[864,128]{1,0:T(8,128)(2,1)S(1)}, bf16[864,128]{1,0:T(8,128)(2,1)S(1)}, u32[]{:S(2)}, u32[]{:S(2)}) collective-permute-start(bf16[864,128]{1,0:T(8,128)(2,1)S(1)} %get-tuple-element.44.refs_4_), channel_id=1, source_target_pairs={{0,4},{4,0},{1,5},{5,1},{2,6},{6,2},{3,7},{7,3},{8,12},{12,8},{9,1... | collective-permute-start | bytes 663560 | tf_op jit(solution)/shard_map/ppermute | solution.py:91
  52.2 11.9 %collective-permute-start.8 = (bf16[128,256]{1,0:T(8,128)(2,1)S(1)}, bf16[128,256]{1,0:T(8,128)(2,1)S(1)}, u32[]{:S(2)}, u32[]{:S(2)}) collective-permute-start(bf16[128,256]{1,0:T(8,128)(2,1)S(1)} %dynamic-slice_convert_fusion.1), channel_id=1, source_target_pairs={{0,16},{8,24},{16,0},{24,8},{1,17},{9,25},{17,1},{25,9},{2,18},{10... | collective-permute-start | bytes 196616 | tf_op jit(solution)/shard_map/ppermute | solution.py:64
  68.0 11.8 %collective-permute-start.4 = (bf16[128,512]{1,0:T(8,128)(2,1)S(1)}, bf16[128,512]{1,0:T(8,128)(2,1)S(1)}, u32[]{:S(2)}, u32[]{:S(2)}) collective-permute-start(bf16[128,512]{1,0:T(8,128)(2,1)S(1)} %fusion.23), channel_id=1, source_target_pairs={{0,16},{8,24},{16,0},{24,8},{1,17},{9,25},{17,1},{25,9},{2,18},{10... | collective-permute-start | bytes 393224 | tf_op jit(solution)/shard_map/ppermute | solution.py:64
  68.0 11.8 %collective-permute-start.3 = (bf16[128,512]{1,0:T(8,128)(2,1)S(1)}, bf16[128,512]{1,0:T(8,128)(2,1)S(1)}, u32[]{:S(2)}, u32[]{:S(2)}) collective-permute-start(bf16[128,512]{1,0:T(8,128)(2,1)S(1)} %fusion.23), channel_id=1, source_target_pairs={{0,8},{8,16},{16,24},{24,0},{1,9},{9,17},{17,25},{25,1},{2,10},{10... | collective-permute-start | bytes 393224 | tf_op jit(solution)/shard_map/ppermute | solution.py:64
  73.0 36.6 %collective-permute-start.11 = (bf16[512,512]{1,0:T(8,128)(2,1)S(1)}, bf16[512,512]{1,0:T(8,128)(2,1)S(1)}, u32[]{:S(2)}, u32[]{:S(2)}) collective-permute-start(bf16[512,512]{1,0:T(8,128)(2,1)S(1)} %pad_maximum_fusion.4.refs_2_), channel_id=1, source_target_pairs={{0,1},{1,0},{2,3},{3,2},{4,5},{5,4},{6,7},{7,6},{8,9},{9,8},{10,11... | collective-permute-start | bytes 1572872 | tf_op jit(solution)/shard_map/ppermute | solution.py:91
  79.8 29.8 %collective-permute-start.6 = (bf16[512,512]{1,0:T(8,128)(2,1)S(1)}, bf16[512,512]{1,0:T(8,128)(2,1)S(1)}, u32[]{:S(2)}, u32[]{:S(2)}) collective-permute-start(bf16[512,512]{1,0:T(8,128)(2,1)S(1)} %pad_maximum_fusion.3.refs_0_), channel_id=1, source_target_pairs={{0,1},{1,0},{2,3},{3,2},{4,5},{5,4},{6,7},{7,6},{8,9},{9,8},{10,11... | collective-permute-start | bytes 1572872 | tf_op jit(solution)/shard_map/ppermute | solution.py:91
  79.9 10.3 %collective-permute-start.12 = (bf16[864,128]{1,0:T(8,128)(2,1)S(1)}, bf16[864,128]{1,0:T(8,128)(2,1)S(1)}, u32[]{:S(2)}, u32[]{:S(2)}) collective-permute-start(bf16[864,128]{1,0:T(8,128)(2,1)S(1)} %copy-done.42), channel_id=1, source_target_pairs={{0,8},{8,16},{16,24},{24,0},{1,9},{9,17},{17,25},{25,1},{2,10},{10... | collective-permute-start | bytes 663560 | tf_op jit(solution)/shard_map/ppermute | solution.py:64
  80.3 18.7 %collective-permute-start.13 = (bf16[864,128]{1,0:T(8,128)(2,1)S(1)}, bf16[864,128]{1,0:T(8,128)(2,1)S(1)}, u32[]{:S(2)}, u32[]{:S(2)}) collective-permute-start(bf16[864,128]{1,0:T(8,128)(2,1)S(1)} %copy-done.41), channel_id=1, source_target_pairs={{0,16},{8,24},{16,0},{24,8},{1,17},{9,25},{17,1},{25,9},{2,18},{10... | collective-permute-start | bytes 663560 | tf_op jit(solution)/shard_map/ppermute | solution.py:64
  82.3 17.1 %collective-permute-start.14 = (bf16[864,128]{1,0:T(8,128)(2,1)S(1)}, bf16[864,128]{1,0:T(8,128)(2,1)S(1)}, u32[]{:S(2)}, u32[]{:S(2)}) collective-permute-start(bf16[864,128]{1,0:T(8,128)(2,1)S(1)} %copy-done.40), channel_id=1, source_target_pairs={{0,24},{8,0},{16,8},{24,16},{1,25},{9,1},{17,9},{25,17},{2,26},{10... | collective-permute-start | bytes 663560 | tf_op jit(solution)/shard_map/ppermute | solution.py:64
  90.2 10.9 %collective-permute-start.16 = (bf16[864,128]{1,0:T(8,128)(2,1)S(1)}, bf16[864,128]{1,0:T(8,128)(2,1)S(1)}, u32[]{:S(2)}, u32[]{:S(2)}) collective-permute-start(bf16[864,128]{1,0:T(8,128)(2,1)S(1)} %collective-permute-done.12.refs_5_), channel_id=1, source_target_pairs={{0,4},{4,0},{1,5},{5,1},{2,6},{6,2},{3,7},{7,3},{8,12},{12,8},{9,1... | collective-permute-start | bytes 663560 | tf_op jit(solution)/shard_map/ppermute | solution.py:91
  119.1 19.3 %collective-permute-start.26 = (bf16[4,2,128,256]{3,2,1,0:T(8,128)(2,1)S(1)}, bf16[4,2,128,256]{3,2,1,0:T(8,128)(2,1)S(1)}, u32[]{:S(2)}, u32[]{:S(2)}) collective-permute-start(bf16[4,2,128,256]{3,2,1,0:T(8,128)(2,1)S(1)} %get-tuple-element.51), channel_id=1, source_target_pairs={{0,1},{1,0},{2,3},{3,2},{4,5},{5,4},{6,7},{7,6},{8,9},{9,8},{10,11... | collective-permute-start | bytes 1572872 | tf_op jit(solution)/shard_map/ppermute | solution.py:91
  119.5 26.7 %collective-permute-start.36 = (bf16[4,864,128]{2,1,0:T(8,128)(2,1)}, bf16[4,864,128]{2,1,0:T(8,128)(2,1)}, u32[]{:S(2)}, u32[]{:S(2)}) collective-permute-start(bf16[4,864,128]{2,1,0:T(8,128)(2,1)} %get-tuple-element.53), channel_id=1, source_target_pairs={{0,4},{4,0},{1,5},{5,1},{2,6},{6,2},{3,7},{7,3},{8,12},{12,8},{9,1... | collective-permute-start | bytes 2654216 | tf_op jit(solution)/shard_map/ppermute | solution.py:91
  129.9 14.1 %collective-permute-start.23 = (bf16[128,256]{1,0:T(8,128)(2,1)S(1)}, bf16[128,256]{1,0:T(8,128)(2,1)S(1)}, u32[]{:S(2)}, u32[]{:S(2)}) collective-permute-start(bf16[128,256]{1,0:T(8,128)(2,1)S(1)} %get-tuple-element.124), channel_id=1, source_target_pairs={{0,24},{8,0},{16,8},{24,16},{1,25},{9,1},{17,9},{25,17},{2,26},{10... | collective-permute-start | bytes 196616 | tf_op jit(solution)/shard_map/ppermute | solution.py:64
  139.3 37.3 %all-to-all-start.2 = ((bf16[8,128,256]{2,1,0:T(8,128)(2,1)}), bf16[8,128,256]{2,1,0:T(8,128)(2,1)S(1)}, u32[]{:S(2)}, u32[]{:S(2)}) async-start(bf16[8,128,256]{2,1,0:T(8,128)(2,1)} %bitcast.50), calls=%async_computation.2 | async-start | bytes 1048576 | tf_op jit(solution)/shard_map/all_to_all | solution.py:59
  150.1 10.6 %collective-permute-start.39 = (bf16[864,128]{1,0:T(8,128)(2,1)S(1)}, bf16[864,128]{1,0:T(8,128)(2,1)S(1)}, u32[]{:S(2)}, u32[]{:S(2)}) collective-permute-start(bf16[864,128]{1,0:T(8,128)(2,1)S(1)} %get-tuple-element.98), channel_id=1, source_target_pairs={{0,24},{8,0},{16,8},{24,16},{1,25},{9,1},{17,9},{25,17},{2,26},{10... | collective-permute-start | bytes 663560 | tf_op jit(solution)/shard_map/ppermute | solution.py:64
  154.1 22.3 %collective-permute-start.38 = (bf16[864,128]{1,0:T(8,128)(2,1)S(1)}, bf16[864,128]{1,0:T(8,128)(2,1)S(1)}, u32[]{:S(2)}, u32[]{:S(2)}) collective-permute-start(bf16[864,128]{1,0:T(8,128)(2,1)S(1)} %get-tuple-element.99), channel_id=1, source_target_pairs={{0,16},{8,24},{16,0},{24,8},{1,17},{9,25},{17,1},{25,9},{2,18},{10... | collective-permute-start | bytes 663560 | tf_op jit(solution)/shard_map/ppermute | solution.py:64
  154.6 21.8 %collective-permute-start.37 = (bf16[864,128]{1,0:T(8,128)(2,1)S(1)}, bf16[864,128]{1,0:T(8,128)(2,1)S(1)}, u32[]{:S(2)}, u32[]{:S(2)}) collective-permute-start(bf16[864,128]{1,0:T(8,128)(2,1)S(1)} %get-tuple-element.100), channel_id=1, source_target_pairs={{0,8},{8,16},{16,24},{24,0},{1,9},{9,17},{17,25},{25,1},{2,10},{10... | collective-permute-start | bytes 663560 | tf_op jit(solution)/shard_map/ppermute | solution.py:64
  198.3 23.3 %collective-permute-start.33 = (bf16[2,512,128]{2,1,0:T(8,128)(2,1)S(1)}, bf16[2,512,128]{2,1,0:T(8,128)(2,1)S(1)}, u32[]{:S(2)}, u32[]{:S(2)}) collective-permute-start(bf16[2,512,128]{2,1,0:T(8,128)(2,1)S(1)} %get-tuple-element.92), channel_id=1, source_target_pairs={{0,16},{8,24},{16,0},{24,8},{1,17},{9,25},{17,1},{25,9},{2,18},{10... | collective-permute-start | bytes 786440 | tf_op jit(solution)/shard_map/ppermute | solution.py:64
  198.6 22.9 %collective-permute-start.32 = (bf16[2,512,128]{2,1,0:T(8,128)(2,1)S(1)}, bf16[2,512,128]{2,1,0:T(8,128)(2,1)S(1)}, u32[]{:S(2)}, u32[]{:S(2)}) collective-permute-start(bf16[2,512,128]{2,1,0:T(8,128)(2,1)S(1)} %get-tuple-element.90), channel_id=1, source_target_pairs={{0,8},{8,16},{16,24},{24,0},{1,9},{9,17},{17,25},{25,1},{2,10},{10... | collective-permute-start | bytes 786440 | tf_op jit(solution)/shard_map/ppermute | solution.py:64
  224.4 12.8 %all-to-all-start.3 = ((bf16[8,128,256]{2,1,0:T(8,128)(2,1)}), bf16[8,128,256]{2,1,0:T(8,128)(2,1)S(1)}, u32[]{:S(2)}, u32[]{:S(2)}) async-start(bf16[8,128,256]{2,1,0:T(8,128)(2,1)} %bitcast.61), calls=%async_computation.3 | async-start | bytes 1048576 | tf_op jit(solution)/shard_map/all_to_all | solution.py:59
  244.1 10.4 %all-to-all-start.4 = ((f32[8,1,640]{2,1,0:T(1,128)}), f32[8,1,640]{2,1,0:T(1,128)S(1)}, u32[]{:S(2)}, u32[]{:S(2)}) async-start(f32[8,1,640]{2,1,0:T(1,128)} %all_to_all.22), calls=%async_computation.4 | async-start | bytes 40960 | tf_op jit(solution)/shard_map/all_to_all | solution.py:59
  (92 other events, 625.3 us)
